TPU v7x, 32 devices: a whole 2x2x4 slice. The times are simulated.
32 devices in a mesh: cfg: 2 (over y), tm: 16 (over z, x, core).
Axes of the slice: x: 2, y: 2, z: 4, core: 2. Of those that a mesh axis runs over, the one named last changes fastest.
Arguments:
- meson_fields: bfloat16 [2, 32, 32, 256, 256], P(None, None, ('cfg', 'tm')), parts along dimension 2, may hold values from -1.3 to 1.3
- perambulators: bfloat16 [2, 32, 256, 256], P(None, ('cfg', 'tm')), parts along dimension 1, may hold values from -0.25 to 0.25
- direct_ins: int32 [4096, 4], replicated, may hold values from 0 to 31, as said below
- direct_coef: float32 [4096], replicated, may hold values from -5 to 5
- direct_entry: int32 [4096], replicated, may hold values from 0 to 63
- box_ins: int32 [8, 4], replicated, may hold values from 0 to 31, as said below
- box_coef: float32 [8], replicated, may hold values from -24 to 24
- box_entry: int32 [8], replicated, may hold values from 0 to 63
Outputs:
- correlator: float32 [3, 2, 128], P(None, None, ('cfg', 'tm')), parts along dimension 2
There are 2 independent parts, one for each index of `cfg`. A program takes and returns all parts, laid end to end along the dimension named above; an argument that names none is the same for every part. Nothing has to cross between parts.
Inputs may be any that keep to these rules, and one draw needn't show every extreme that they name: `direct_ins`: within a term, insertions 0 and 1 differ, 1 and 2 differ, 2 and 3 differ. `box_ins`: within a term, insertions 0 and 1 differ, 1 and 2 differ, 2 and 3 differ.
All inputs are finite; a program needn't handle non-finite values.
Results may differ from a plain program's by a relative error of at most 0.0046.
Values may be sent and summed in bfloat16 or wider, within the bound.
No kernel may reach another device: no remote copies, remote signals or barrier semaphores. Data moves between devices by JAX's collectives and lax.ppermute only.
A program may use at most 192 MiB of HBM per device.

v0:
```python
import functools

import jax
import jax.numpy as jnp
from jax import lax
from jax.experimental import pallas as pl
from jax.experimental.pallas import tpu as pltpu
from jax.sharding import PartitionSpec as P

CHUNKS = 4
GROUP = 4
STEP_ROWS = 16
STEP_INS = 8
TERM_STEP = 512
NT = (((1,), (1,)), ((), ()))


def nt_dot(left, right):
    return lax.dot_general(left, right, NT, preferred_element_type=jnp.float32)


def dress_kernel(fields, factor, *refs):
    outs, weight = refs[:-1], refs[-1]
    modes = factor.shape[-1]
    step = pl.program_id(0)

    @pl.when(step == 0)
    def _():
        weight[:modes, :modes] = factor[0]
        weight[:modes, modes:] = factor[1]
        weight[modes:, :modes] = -factor[1]
        weight[modes:, modes:] = factor[0]

    inserts, rows = fields.shape[1:3]
    sides = fields[...].reshape(2, inserts * rows, modes)
    product = jnp.dot(
        jnp.concatenate([sides[0], sides[1]], axis=1),
        weight[...],
        preferred_element_type=jnp.float32,
    )
    steps = pl.num_programs(0) // len(outs)
    for number, out in enumerate(outs):

        @pl.when(step // steps == number)
        def _(out=out):
            out[0] = product[:, :modes].reshape(inserts, rows, modes).astype(out.dtype)
            out[1] = product[:, modes:].reshape(inserts, rows, modes).astype(out.dtype)


def dress(fields, factor, first, count):
    inserts, modes = fields.shape[1], fields.shape[-1]
    rows = modes // CHUNKS
    steps = inserts // STEP_INS
    block = (2, STEP_INS, rows, modes)

    def place(number):
        return lambda g: (0, jnp.clip(g - number * steps, 0, steps - 1), 0, 0)

    return pl.pallas_call(
        dress_kernel,
        grid=(count * steps,),
        in_specs=[
            pl.BlockSpec(block, lambda g: (0, g % steps, first + g // steps, 0)),
            pl.BlockSpec((2, modes, modes), lambda g: (0, 0, 0)),
        ],
        out_specs=[pl.BlockSpec(block, place(number)) for number in range(count)],
        out_shape=[jax.ShapeDtypeStruct((2, inserts, rows, modes), fields.dtype)] * count,
        scratch_shapes=[pltpu.VMEM((2 * modes, 2 * modes), fields.dtype)],
        cost_estimate=pl.CostEstimate(
            flops=16 * count * inserts * rows * modes * modes,
            bytes_accessed=8 * count * inserts * rows * modes,
            transcendentals=0,
        ),
        name="dress",
    )(fields, factor)


def gram_kernel(count, left_count, *refs):
    blocks, before, out, flat = refs[:count], refs[count], refs[count + 1], refs[count + 2]
    _, inserts, rows, modes = blocks[0].shape
    size = 2 * inserts
    for index, block in enumerate(blocks):
        flat[index * size : (index + 1) * size] = block[...].reshape(size, rows * modes)
    product = nt_dot(flat[: left_count * size], flat[(count - out.shape[1] // size) * size :])

    @pl.when(pl.program_id(0) == 0)
    def _():
        out[...] = before[...] + product

    @pl.when(pl.program_id(0) > 0)
    def _():
        out[...] += product


def gram(blocks, left_count, right_count, before):
    count = len(blocks)
    _, inserts, rows, modes = blocks[0].shape
    size = 2 * inserts
    spec = pl.BlockSpec((2, inserts, STEP_ROWS, modes), lambda i: (0, 0, i, 0))
    shape = (left_count * size, right_count * size)
    whole = pl.BlockSpec(shape, lambda i: (0, 0))
    return pl.pallas_call(
        functools.partial(gram_kernel, count, left_count),
        grid=(rows // STEP_ROWS,),
        in_specs=[spec] * count + [whole],
        out_specs=whole,
        out_shape=jax.ShapeDtypeStruct(shape, jnp.float32),
        scratch_shapes=[pltpu.VMEM((count * size, STEP_ROWS * modes), jnp.bfloat16)],
        cost_estimate=pl.CostEstimate(
            flops=16 * shape[0] * shape[1] * rows * modes,
            bytes_accessed=count * 2 * size * rows * modes,
            transcendentals=0,
        ),
        name="gram",
    )(*blocks, before)


def box_kernel(left_count, right_count, ins, entry, coef, weight, before, *refs):
    left, refs = refs[:left_count], refs[left_count:]
    right, refs = refs[:right_count], refs[right_count:]
    extra, (out, held, sems) = refs[:-3], refs[-3:]
    terms = held.shape[0]
    rows = left[0].shape[2]

    @pl.loop(0, terms)
    def _(term):
        for place in range(4):
            where = ins[place, term]
            sources = [ref.at[:, where] for ref in (right if place % 2 else left)]
            if place % 2 == 0:
                for ref in extra:
                    where = (place // 2) * terms + term
                    sources += [ref.at[number, :, where] for number in range(ref.shape[0])]
            for number, source in enumerate(sources):
                pltpu.make_async_copy(
                    source,
                    held.at[term, place, :, pl.ds(number * rows, rows)],
                    sems.at[term],
                ).start()

    def product(term, one, other):
        real, imag = held[term, one, 0], held[term, one, 1]
        other_side = jnp.concatenate([held[term, other, 0], held[term, other, 1]], axis=1)
        return (
            nt_dot(jnp.concatenate([real, imag], axis=1), other_side),
            nt_dot(jnp.concatenate([imag, -real], axis=1), other_side),
        )

    out[...] = before[...]
    spot = lax.broadcasted_iota(jnp.int32, out.shape, 1)
    line = lax.broadcasted_iota(jnp.int32, out.shape, 0)

    @pl.loop(0, terms)
    def _(term):
        pltpu.make_async_copy(held.at[term], held.at[term], sems.at[term]).wait()
        first_real, first_imag = product(term, 0, 1)
        second_real, second_imag = product(term, 3, 2)
        real = jnp.sum(first_real * second_real + first_imag * second_imag) * coef[term]
        imag = jnp.sum(first_imag * second_real - first_real * second_imag) * coef[term]
        imag = imag * weight[3]
        added = jnp.zeros(out.shape, jnp.float32)
        for apart in range(3):
            added = jnp.where(line == 2 * apart, real * weight[apart], added)
            added = jnp.where(line == 2 * apart + 1, imag * weight[apart], added)
        out[...] -= jnp.where(spot == entry[term], added, 0.0)


def box(left, right, ins, entry, coef, weight, before, extra=None):
    extra = [] if extra is None else [extra]
    terms = ins.shape[1]
    modes = left[0].shape[3]
    count = len(left) + len(right) + len(extra)
    smem = pl.BlockSpec(memory_space=pltpu.SMEM)
    vmem = pl.BlockSpec(memory_space=pltpu.VMEM)
    return pl.pallas_call(
        functools.partial(box_kernel, len(left), len(right)),
        in_specs=[smem] * 4 + [vmem] + [pl.BlockSpec(memory_space=pl.ANY)] * count,
        out_specs=vmem,
        out_shape=jax.ShapeDtypeStruct(before.shape, jnp.float32),
        scratch_shapes=[
            pltpu.VMEM((terms, 4, 2, modes, modes), left[0].dtype),
            pltpu.SemaphoreType.DMA((terms,)),
        ],
        cost_estimate=pl.CostEstimate(
            flops=32 * terms * modes * modes * modes,
            bytes_accessed=16 * terms * modes * modes,
            transcendentals=0,
        ),
        name="box",
    )(ins, entry, coef, weight, before, *left, *right, *extra)


def pick_kernel(upper, ins, *refs):
    del ins
    blocks, out = refs[:-1], refs[-1]
    half = len(blocks) // 2

    @pl.when(upper[0] == 1)
    def _():
        for number in range(half):
            out[number] = blocks[half + number][...]

    @pl.when(upper[0] == 0)
    def _():
        for number in range(half):
            out[number] = blocks[number][...]


def pick(blocks, places, upper):
    _, _, rows, modes = blocks[0].shape
    half, count = len(blocks) // 2, places.shape[0]
    spec = pl.BlockSpec((2, 1, rows, modes), lambda l, upper, ins: (0, ins[l], 0, 0))
    return pl.pallas_call(
        pick_kernel,
        grid_spec=pltpu.PrefetchScalarGridSpec(
            num_scalar_prefetch=2,
            grid=(count,),
            in_specs=[spec] * len(blocks),
            out_specs=pl.BlockSpec(
                (half, 2, 1, rows, modes), lambda l, upper, ins: (0, 0, l, 0, 0)
            ),
        ),
        out_shape=jax.ShapeDtypeStruct((half, 2, count, rows, modes), blocks[0].dtype),
        name="pick",
    )(upper, places, *blocks)


def thirds(value, axis):
    high = value.astype(jnp.bfloat16)
    rest = value - high.astype(jnp.float32)
    middle = rest.astype(jnp.bfloat16)
    low = (rest - middle.astype(jnp.float32)).astype(jnp.bfloat16)
    return jnp.concatenate([high, middle, low], axis=axis)


def direct_kernel(swap, weight, ins, coef, entry, before, *refs):
    tables, out, lines = refs[:-2], refs[-2], refs[-1]
    size = 2 * lines.shape[1]
    inserts = size // 2
    if len(tables) == 1:
        grams = [tables[0][:size, place * size : (place + 1) * size] for place in range(3)]
        below = tables[0][size:, 2 * size :]
        grams[2] = jnp.where(swap[3] == 1, below, grams[2])
    else:
        grams = [tables[0][...] + tables[1][...].T]
    pairs = len(grams)
    for pair, table in enumerate(grams):
        table = jnp.where(swap[pair] == 1, table.T, table)
        upper, lower = table[:inserts], table[inserts:]
        lines[pair * size : pair * size + inserts] = upper[:, :inserts] + lower[:, inserts:]
        lines[pair * size + inserts : (pair + 1) * size] = lower[:, :inserts] - upper[:, inserts:]
    table = thirds(lines[...], 1)
    entries = out.shape[1]
    total = before[...]
    step = min(TERM_STEP, ins.shape[1])
    for start in range(0, ins.shape[1], step):
        span = slice(start, start + step)
        places = lax.broadcasted_iota(jnp.int32, (inserts, step), 0)

        def values(left, right):
            chosen = (places == ins[right : right + 1, span]).astype(jnp.bfloat16)
            chosen = jnp.concatenate([chosen] * 3, axis=0)
            picked = jnp.dot(table, chosen, preferred_element_type=jnp.float32)
            here = places == ins[left : left + 1, span]
            return [
                jnp.sum(
                    jnp.where(here, picked[part * inserts : (part + 1) * inserts], 0.0),
                    axis=0,
                    keepdims=True,
                )
                for part in range(2 * pairs)
            ]

        first, second = values(0, 1), values(2, 3)
        scale = coef[:, span]
        sums = [jnp.zeros((1, step), jnp.float32) for _ in range(8)]
        for pair in range(pairs):
            a, b = first[2 * pair], first[2 * pair + 1]
            c, d = second[2 * pair], second[2 * pair + 1]
            real, imag = scale * (a * c - b * d), scale * (a * d + b * c)
            for apart in range(3):
                sums[2 * apart] += weight[3 * pair + apart] * real
                sums[2 * apart + 1] += weight[3 * pair + apart] * imag
        rows = thirds(jnp.concatenate(sums, axis=0), 0)
        bins = lax.broadcasted_iota(jnp.int32, (entries, step), 0)
        bins = (bins == entry[:, span]).astype(jnp.bfloat16)
        spread = nt_dot(rows, bins)
        total += spread[:8] + spread[8:16] + spread[16:]
    out[...] = total


def direct(tables, pairs, swap, weight, ins, coef, entry, before):
    size = tables[0].shape[0] // (2 if pairs == 3 else 1)
    smem = pl.BlockSpec(memory_space=pltpu.SMEM)
    vmem = pl.BlockSpec(memory_space=pltpu.VMEM)
    return pl.pallas_call(
        direct_kernel,
        in_specs=[smem, smem] + [vmem] * (4 + len(tables)),
        out_specs=vmem,
        out_shape=jax.ShapeDtypeStruct(before.shape, jnp.float32),
        scratch_shapes=[pltpu.VMEM((pairs * size, size // 2), jnp.float32)],
        cost_estimate=pl.CostEstimate(
            flops=2 * pairs * size * size * ins.shape[1] * 3,
            bytes_accessed=40 * ins.shape[1],
            transcendentals=0,
        ),
        name="direct",
    )(swap, weight, ins, coef, entry, before, *tables)


def after(value, *others):
    return lax.optimization_barrier((value,) + others)[0]


def total_over(value, axis):
    devices = lax.axis_size(axis)
    if devices & (devices - 1):
        return lax.psum(value, axis)
    distance = 1
    while distance < devices:
        value = value + lax.ppermute(value, axis, [(i, i ^ distance) for i in range(devices)])
        distance *= 2
    return value


def local(
    meson_fields, perambulators, direct_ins, direct_coef, direct_entry, box_ins, box_coef, box_entry
):
    devices = lax.axis_size("tm")
    owned = 4
    entries = owned * devices
    here = lax.axis_index("tm")
    role = here % GROUP
    everyone = range(devices)

    def move(value, target):
        route = [(i, target[i % GROUP](i) % devices) for i in everyone if i % GROUP in target]
        return lax.ppermute(value, "tm", route)

    def by_role(*choices):
        picked = jnp.asarray(choices[3])
        for number in range(3):
            picked = jnp.where(role == number, choices[number], picked)
        return picked

    fields = meson_fields[:, :, 0]
    factor = perambulators[:, 0]
    own = dress(fields, factor, 0, 1) + dress(fields, factor, 1, CHUNKS - 1)
    half = CHUNKS // 2

    across = {0: lambda i: i + 1, 1: lambda i: i + 2, 2: lambda i: i - 2, 3: lambda i: i - 1}
    along = {0: lambda i: i - GROUP, 3: lambda i: i + GROUP}
    beside = {0: lambda i: i + 1, 3: lambda i: i - 1}
    cross = {0: lambda i: i + 2, 3: lambda i: i - 2}

    terms = box_ins.shape[0]
    ins_table = box_ins.T
    swapped_table = ins_table[jnp.array([1, 0, 3, 2])]
    part = terms // 2
    late_table = jnp.where(role == 1, ins_table[:, part:], swapped_table[:, :part])
    send_table = jnp.where(role == 0, swapped_table[:, :part], ins_table[:, part:])
    late_entry = jnp.where(role == 1, box_entry[part:], box_entry[:part])
    late_coef = jnp.where(role == 1, box_coef[part:], box_coef[:part])

    near, far = [], []
    for chunk in range(CHUNKS):
        near.append(move(own[chunk], across))
        far.append(move(own[chunk], along))
    split = [jnp.where(role == 0, own[half + j], own[j]) for j in range(half)]
    chosen = jnp.concatenate([send_table[0], send_table[2]])
    extra = pick(own, chosen, jnp.where(role == 0, 0, 1).astype(jnp.int32)[None])
    split_in = []
    for piece in split:
        split_in.append(move(after(piece, near[CHUNKS - 2]), cross))
    extra_in = move(after(extra, near[CHUNKS - 2]), cross)

    edge = (role == 0) | (role == 3)
    one, zero = jnp.float32(1.0), jnp.float32(0.0)

    def weights(first, second, third):
        return jnp.stack([first + zero, second + zero, third + zero])

    def with_sign(weight, swap):
        return jnp.concatenate([weight, jnp.where(swap == 1, -one, one)[None]])

    def role_table(swap):
        return jnp.where(swap == 1, swapped_table, ins_table)

    outer = jnp.where(edge, one, zero)
    inner = one - outer
    same_weight = weights(one, zero, zero)
    near_weight = weights(zero, inner, outer)
    third_weight = weights(zero, by_role(zero, zero, one, zero), outer)
    split_weight = weights(zero, by_role(zero, one, zero, zero), zero)
    both_inner = weights(zero, inner, zero)
    near_swap = by_role(0, 1, 0, 1)
    third_swap = by_role(0, 0, 1, 1)
    size = 2 * fields.shape[1]

    total = box(
        own, own, ins_table, box_entry, box_coef, with_sign(same_weight, 0),
        jnp.zeros((8, entries), jnp.float32),
    )
    table = jnp.zeros((2 * size, 3 * size), jnp.float32)
    early = (total, extra) + tuple(split)
    near_beside = []
    for chunk in range(CHUNKS):
        near_beside.append(move(after(near[chunk], *early), beside))
        table = lax.cond(
            edge,
            lambda o, a, z, c, t: gram([o, a, z], 2, 3, t),
            lambda o, a, z, c, t: gram([o, a, c], 2, 3, t),
            own[chunk], near[chunk], far[chunk], near_beside[chunk], table,
        )
        early = (table,)
    far_beside = [move(after(piece, table), beside) for piece in far]
    total = after(total, table)
    total = box(
        own, near, role_table(near_swap), box_entry, box_coef,
        with_sign(near_weight, near_swap), total,
    )
    total = lax.cond(
        edge,
        lambda o, a, z, c, *rest: box(a, z, *rest),
        lambda o, a, z, c, *rest: box(o, c, *rest),
        own, near, far, near_beside, role_table(third_swap), box_entry, box_coef,
        with_sign(third_weight, third_swap), total,
    )
    direct_table = direct_ins.T
    total = direct(
        [table], 3,
        jnp.stack([jnp.int32(0), near_swap, third_swap, edge.astype(jnp.int32)]),
        jnp.concatenate([same_weight, near_weight, third_weight]),
        direct_table, direct_coef[None], direct_entry[None], total,
    )
    split_gram = after(jnp.zeros((size, size), jnp.float32), total)
    for j in range(half):
        split_gram = lax.cond(
            role == 1,
            lambda v, lo, hi, t: gram([v, lo], 1, 1, t),
            lambda v, lo, hi, t: gram([v, hi], 1, 1, t),
            split_in[j], far_beside[j], far_beside[half + j], split_gram,
        )
    split_other = move(split_gram, {2: lambda i: i - 5})
    total = direct(
        [split_gram, split_other], 1, jnp.zeros((4,), jnp.int32), split_weight,
        direct_table, direct_coef[None], direct_entry[None], total,
    )
    total = lax.cond(
        role == 1,
        lambda v, x, f, *rest: box(v, f, *rest, extra=x),
        lambda v, x, f, *rest: box(v, f[half:] + f[:half], *rest, extra=x),
        split_in, extra_in, far_beside, late_table, late_entry, late_coef,
        with_sign(both_inner, by_role(0, 0, 1, 0)), total,
    )
    summed = total_over(total, "tm") / devices
    mine = lax.dynamic_slice_in_dim(summed[:6], here * owned, owned, axis=1)
    return mine.reshape(3, 2, owned)


def solution(mesh):
    placed = (
        P(None, None, ("cfg", "tm"), None, None),
        P(None, ("cfg", "tm"), None, None),
        P(),
        P(),
        P(),
        P(),
        P(),
        P(),
    )

    return jax.shard_map(
        local, mesh=mesh, in_specs=placed, out_specs=P(None, None, ("cfg", "tm")), check_vma=False
    )
```

profile of v0, /device:TPU:0, one launch (start us, length us, event | category | flops | bytes accessed | tf_op | source)
XLA Modules:
  0.0 217.1 jit_solution(9822185810496895033)
XLA Ops:
  0.0 3.9 %dress.2.refs_0_.refs_4_ = bf16[2,32,64,256]{3,2,1,0:T(8,128)(2,1)S(1)} custom-call(bf16[2,32,256,256]{3,2,1,0:T(8,128)(2,1)} %bitcast.24, bf16[2,256,256]{2,1,0:T(8,128)(2,1)} %bitcast.26), custom_call_target="tpu_custom_call" | custom-call | flops 2147483648 | bytes 4194304 | tf_op jit(solution)/shard_map/dress/pallas_call | solution.py:59
  4.5 6.5 %collective-permute-start.5 = (bf16[2,32,64,256]{3,2,1,0:T(8,128)(2,1)S(1)}, bf16[2,32,64,256]{3,2,1,0:T(8,128)(2,1)}, u32[]{:S(2)}, u32[]{:S(2)}) collective-permute-start(bf16[2,32,64,256]{3,2,1,0:T(8,128)(2,1)S(1)} %dress.2.refs_0_.refs_4_), channel_id=1, source_target_pairs={{0,12},{3,7},{4,0},{7,11},{8,4},{11,15},{12,8},{15,3},{16,28},{19,... | collective-permute-start | bytes 6291464 | tf_op jit(solution)/shard_map/ppermute | solution.py:338
  12.3 12.3 %dress.3 = (bf16[2,32,64,256]{3,2,1,0:T(8,128)(2,1)}, bf16[2,32,64,256]{3,2,1,0:T(8,128)(2,1)}, bf16[2,32,64,256]{3,2,1,0:T(8,128)(2,1)}) custom-call(bf16[2,32,256,256]{3,2,1,0:T(8,128)(2,1)} %bitcast.25, bf16[2,256,256]{2,1,0:T(8,128)(2,1)} %bitcast.27), custom_call_target="tpu_custom_call" | custom-call | flops 6442450944 | bytes 12582912 | tf_op jit(solution)/shard_map/dress/pallas_call | solution.py:59
  24.7 5.9 %pick.1 = bf16[2,2,8,64,256]{4,3,2,1,0:T(8,128)(2,1)} custom-call(s32[1]{0:T(128)} %bitcast.16.upper, s32[8]{0:T(128)} %pad_add_fusion.1.ins, bf16[2,32,64,256]{3,2,1,0:T(8,128)(2,1)S(1)} %dress.2.refs_0_.refs_4_, bf16[2,32,64,256]{3,2,1,0:T(8,128)(2,1)} %get-tuple-element.321.refs_1_.refs_5_, bf16[2,32,64,256]{3,2,1,0:T(8,128)(2,1)} %get-tuple-element.322.refs_2_.refs_6_, ...), custom_call_target="tpu_custom_call" | custom-call | tf_op jit(solution)/shard_map/pick/pallas_call | solution.py:213
  36.1 7.9 %box.10.before = f32[8,64]{1,0:T(8,128)} custom-call(s32[4,8]{1,0:T(4,128)} %bitcast.28, s32[8]{0:T(128)S(1)} %copy-done.4, f32[8]{0:T(128)S(1)} %copy-done.5, f32[4]{0:T(128)} %constant.51.clone.1.weight, f32[8,64]{1,0:T(8,128)} %broadcast_in_dim.42.before, bf16[2,32,64,256]{3,2,1,0:T(8,128)(2,1)S(1)} %dress.2.refs_0_.refs_4_, ...), custom_call_target="tpu_custom_call" | custom-call | flops 4294967296 | bytes 8388608 | tf_op jit(solution)/shard_map/box/pallas_call | solution.py:175
  49.9 5.9 %conditional.8 = (f32[128,192]{1,0:T(8,128)S(1)}) conditional(s32[]{:T(128)} %convert_element_type.5, (bf16[2,32,64,256]{3,2,1,0:T(8,128)(2,1)S(1)}, bf16[2,32,64,256]{3,2,1,0:T(8,128)(2,1)}, bf16[2,32,64,256]{3,2,1,0:T(8,128)(2,1)}) %tuple.67, (bf16[2,32,64,256]{3,2,1,0:T(8,128)(2,1)S(1)}, bf16[2,32,64,256]{3,2,1,0:T(8,128)(2,1)}, ...), branch_computations={%region_0.1_spmd, %region_1.2_spmd} | conditional | flops 6442450944 | bytes 6389772 | solution.py:409
  50.6 5.3 %gram.13 = f32[128,192]{1,0:T(8,128)S(1)} custom-call(bf16[2,32,64,256]{3,2,1,0:T(8,128)(2,1)S(1)} %get-tuple-element.201.refs_0_, bf16[2,32,64,256]{3,2,1,0:T(8,128)(2,1)} %get-tuple-element.202.refs_1_, bf16[2,32,64,256]{3,2,1,0:T(8,128)(2,1)} %get-tuple-element.216.refs_2_, f32[128,192]{1,0:T(8,128)} %broadcast_in_dim.10.refs_3_), custom_call_target="tpu_custom_call" | custom-call | flops 6442450944 | bytes 6291456 | tf_op jit(solution)/shard_map/cond/branch_1_fun/gram/pallas_call | solution.py:102
  55.8 17.1 %collective-permute-done.2.refs_5_ = bf16[2,32,64,256]{3,2,1,0:T(8,128)(2,1)} collective-permute-done((bf16[2,32,64,256]{3,2,1,0:T(8,128)(2,1)}, bf16[2,32,64,256]{3,2,1,0:T(8,128)(2,1)}, u32[]{:S(2)}, u32[]{:S(2)}) %collective-permute-start.2) | collective-permute-done | bytes 2097184 | tf_op jit(solution)/shard_map/ppermute | solution.py:338
  78.8 5.5 %conditional.9 = (f32[128,192]{1,0:T(8,128)S(1)}) conditional(s32[]{:T(128)} %convert_element_type.5, (bf16[2,32,64,256]{3,2,1,0:T(8,128)(2,1)}, bf16[2,32,64,256]{3,2,1,0:T(8,128)(2,1)}, bf16[2,32,64,256]{3,2,1,0:T(8,128)(2,1)}, f32[128,192]{1,0:T(8,128)S(1)}) %tuple.70, (bf16[2,32,64,256]{3,2,1,0:T(8,128)(2,1)}, bf16[2,32,64,256]{3,2,1,0:T(8,128)(2,1)}, ...), branch_computations={%region_2.3_spmd, %region_3.4_spmd} | conditional | flops 6442450944 | bytes 6291464 | solution.py:409
  78.9 5.5 %gram.15 = f32[128,192]{1,0:T(8,128)S(1)} custom-call(bf16[2,32,64,256]{3,2,1,0:T(8,128)(2,1)} %get-tuple-element.223.refs_0_, bf16[2,32,64,256]{3,2,1,0:T(8,128)(2,1)} %get-tuple-element.224.refs_1_, bf16[2,32,64,256]{3,2,1,0:T(8,128)(2,1)} %get-tuple-element.225.refs_2_, f32[128,192]{1,0:T(8,128)S(1)} %get-tuple-element.226.refs_3_), custom_call_target="tpu_custom_call" | custom-call | flops 6442450944 | bytes 6291456 | tf_op jit(solution)/shard_map/cond/branch_1_fun/gram/pallas_call | solution.py:102
  84.4 17.5 %collective-permute-done.1.refs_6_ = bf16[2,32,64,256]{3,2,1,0:T(8,128)(2,1)} collective-permute-done((bf16[2,32,64,256]{3,2,1,0:T(8,128)(2,1)}, bf16[2,32,64,256]{3,2,1,0:T(8,128)(2,1)}, u32[]{:S(2)}, u32[]{:S(2)}) %collective-permute-start.1) | collective-permute-done | bytes 2097184 | tf_op jit(solution)/shard_map/ppermute | solution.py:338
  107.8 5.5 %conditional.10 = (f32[128,192]{1,0:T(8,128)S(1)}) conditional(s32[]{:T(128)} %convert_element_type.5, (bf16[2,32,64,256]{3,2,1,0:T(8,128)(2,1)}, bf16[2,32,64,256]{3,2,1,0:T(8,128)(2,1)}, bf16[2,32,64,256]{3,2,1,0:T(8,128)(2,1)}, f32[128,192]{1,0:T(8,128)S(1)}) %tuple.73, (bf16[2,32,64,256]{3,2,1,0:T(8,128)(2,1)}, ...), branch_computations={%region_4.5_spmd, %region_5.6_spmd} | conditional | flops 6442450944 | bytes 6291464 | solution.py:409
  107.9 5.5 %gram.17 = f32[128,192]{1,0:T(8,128)S(1)} custom-call(bf16[2,32,64,256]{3,2,1,0:T(8,128)(2,1)} %get-tuple-element.231.refs_0_, bf16[2,32,64,256]{3,2,1,0:T(8,128)(2,1)} %get-tuple-element.232.refs_1_, bf16[2,32,64,256]{3,2,1,0:T(8,128)(2,1)} %get-tuple-element.233.refs_2_, f32[128,192]{1,0:T(8,128)S(1)} %get-tuple-element.234.refs_3_), custom_call_target="tpu_custom_call" | custom-call | flops 6442450944 | bytes 6291456 | tf_op jit(solution)/shard_map/cond/branch_1_fun/gram/pallas_call | solution.py:102
  113.4 17.5 %collective-permute-done.refs_7_ = bf16[2,32,64,256]{3,2,1,0:T(8,128)(2,1)} collective-permute-done((bf16[2,32,64,256]{3,2,1,0:T(8,128)(2,1)}, bf16[2,32,64,256]{3,2,1,0:T(8,128)(2,1)}, u32[]{:S(2)}, u32[]{:S(2)}) %collective-permute-start) | collective-permute-done | bytes 2097184 | tf_op jit(solution)/shard_map/ppermute | solution.py:338
  136.3 5.5 %conditional.11 = (f32[128,192]{1,0:T(8,128)S(1)}) conditional(s32[]{:T(128)} %convert_element_type.5, (bf16[2,32,64,256]{3,2,1,0:T(8,128)(2,1)}, bf16[2,32,64,256]{3,2,1,0:T(8,128)(2,1)}, bf16[2,32,64,256]{3,2,1,0:T(8,128)(2,1)}, f32[128,192]{1,0:T(8,128)S(1)}) %tuple.76, (bf16[2,32,64,256]{3,2,1,0:T(8,128)(2,1)}, ...), branch_computations={%region_6.7_spmd, %region_7.8_spmd} | conditional | flops 6442450944 | bytes 6291464 | solution.py:409
  136.3 5.5 %gram.19 = f32[128,192]{1,0:T(8,128)S(1)} custom-call(bf16[2,32,64,256]{3,2,1,0:T(8,128)(2,1)} %get-tuple-element.239.refs_0_, bf16[2,32,64,256]{3,2,1,0:T(8,128)(2,1)} %get-tuple-element.240.refs_1_, bf16[2,32,64,256]{3,2,1,0:T(8,128)(2,1)} %get-tuple-element.241.refs_2_, f32[128,192]{1,0:T(8,128)S(1)} %get-tuple-element.242.refs_3_), custom_call_target="tpu_custom_call" | custom-call | flops 6442450944 | bytes 6291456 | tf_op jit(solution)/shard_map/cond/branch_1_fun/gram/pallas_call | solution.py:102
  153.4 5.3 %collective-permute-done.14 = bf16[2,32,64,256]{3,2,1,0:T(8,128)(2,1)} collective-permute-done((bf16[2,32,64,256]{3,2,1,0:T(8,128)(2,1)}, bf16[2,32,64,256]{3,2,1,0:T(8,128)(2,1)}, u32[]{:S(2)}, u32[]{:S(2)}) %collective-permute-start.14) | collective-permute-done | bytes 2097184 | tf_op jit(solution)/shard_map/ppermute | solution.py:338
  167.0 6.9 %box.11 = f32[8,64]{1,0:T(8,128)S(1)} custom-call(s32[4,8]{1,0:T(4,128)} %get-tuple-element.339.ins, s32[8]{0:T(128)S(1)} %copy-done.4, f32[8]{0:T(128)S(1)} %copy-done.5, f32[4]{0:T(128)} %get-tuple-element.344.weight, f32[8,64]{1,0:T(8,128)} %box.10.before, bf16[2,32,64,256]{3,2,1,0:T(8,128)(2,1)S(1)} %dress.2.refs_0_.refs_4_, ...), custom_call_target="tpu_custom_call" | custom-call | flops 4294967296 | bytes 8388608 | tf_op jit(solution)/shard_map/box/pallas_call | solution.py:175
  173.9 6.9 %conditional.12 = (f32[8,64]{1,0:T(8,128)S(1)}) conditional(s32[]{:T(128)} %convert_element_type.5, (s32[4,8]{1,0:T(4,128)S(1)}, s32[8]{0:T(128)S(1)}, f32[8]{0:T(128)S(1)}, f32[4]{0:T(128)S(1)}, f32[8,64]{1,0:T(8,128)S(1)}, /*index=5*/bf16[2,32,64,256]{3,2,1,0:T(8,128)(2,1)S(1)}, bf16[2,32,64,256]{3,2,1,0:T(8,128)(2,1)}, ...), branch_computations={%region_8.9_spmd, %region_9.10_spmd} | conditional | flops 4294967296 | bytes 8388616 | solution.py:422
  173.9 6.7 %box.7 = f32[8,64]{1,0:T(8,128)S(1)} custom-call(s32[4,8]{1,0:T(4,128)S(1)} %get-tuple-element.256.ins, s32[8]{0:T(128)S(1)} %get-tuple-element.257.entry, f32[8]{0:T(128)S(1)} %get-tuple-element.258.coef, f32[4]{0:T(128)S(1)} %get-tuple-element.259.weight, f32[8,64]{1,0:T(8,128)S(1)} %get-tuple-element.260.before, ...), custom_call_target="tpu_custom_call" | custom-call | flops 4294967296 | bytes 8388608 | tf_op jit(solution)/shard_map/cond/branch_1_fun/box/pallas_call | solution.py:175
  180.8 4.1 %direct.2.before = f32[8,64]{1,0:T(8,128)} custom-call(s32[4]{0:T(128)} %pad_add_fusion.swap, f32[9]{0:T(128)} %concatenate.20.weight, s32[4,4096]{1,0:T(4,128)} %bitcast.32, f32[1,4096]{1,0:T(1,128)} %bitcast.34, s32[1,4096]{1,0:T(1,128)} %bitcast.36, f32[8,64]{1,0:T(8,128)S(1)} %get-tuple-element.351.before, f32[128,192]{1,0:T(8,128)S(1)} %get-tuple-element.350.refs_0_), custom_call_target="tpu_custom_call" | custom-call | flops 301989888 | bytes 163840 | tf_op jit(solution)/shard_map/direct/pallas_call | solution.py:296
  188.9 3.9 %conditional.14 = (f32[64,64]{1,0:T(8,128)S(1)}) conditional(s32[]{:T(128)} %convert_element_type.4, (bf16[2,32,64,256]{3,2,1,0:T(8,128)(2,1)}, bf16[2,32,64,256]{3,2,1,0:T(8,128)(2,1)}, f32[64,64]{1,0:T(8,128)S(1)}) %tuple.89, (bf16[2,32,64,256]{3,2,1,0:T(8,128)(2,1)}, bf16[2,32,64,256]{3,2,1,0:T(8,128)(2,1)}, f32[64,64]{1,0:T(8,128)S(1)}) %tuple.91), branch_computations={%region_12.13_spmd, %region_13.14_spmd} | conditional | flops 1073741824 | bytes 4194312 | solution.py:438
  197.6 4.3 %conditional.15 = (f32[8,64]{1,0:T(8,128)S(1)}) conditional(s32[]{:T(128)} %convert_element_type.4, (s32[4,4]{1,0:T(4,128)S(1)}, s32[4]{0:T(128)S(1)}, f32[4]{0:T(128)S(1)}, f32[4]{0:T(128)S(1)}, f32[8,64]{1,0:T(8,128)S(1)}, /*index=5*/bf16[2,32,64,256]{3,2,1,0:T(8,128)(2,1)}, bf16[2,32,64,256]{3,2,1,0:T(8,128)(2,1)}, ...), branch_computations={%region_14.15_spmd, %region_15.16_spmd} | conditional | flops 2147483648 | bytes 4194312 | solution.py:449
  197.6 4.3 %box.8 = f32[8,64]{1,0:T(8,128)S(1)} custom-call(s32[4,4]{1,0:T(4,128)S(1)} %get-tuple-element.281.ins, s32[4]{0:T(128)S(1)} %get-tuple-element.282.entry, f32[4]{0:T(128)S(1)} %get-tuple-element.283.coef, f32[4]{0:T(128)S(1)} %get-tuple-element.284.weight, f32[8,64]{1,0:T(8,128)S(1)} %get-tuple-element.285.before, ...), custom_call_target="tpu_custom_call" | custom-call | flops 2147483648 | bytes 4194304 | tf_op jit(solution)/shard_map/cond/branch_0_fun/box/pallas_call | solution.py:175
  (89 shorter events, 82.7 us)
Async XLA Ops:
  3.9 40.0 %collective-permute-start.3 = (bf16[2,32,64,256]{3,2,1,0:T(8,128)(2,1)S(1)}, bf16[2,32,64,256]{3,2,1,0:T(8,128)(2,1)}, u32[]{:S(2)}, u32[]{:S(2)}) collective-permute-start(bf16[2,32,64,256]{3,2,1,0:T(8,128)(2,1)S(1)} %dress.2.refs_0_.refs_4_), channel_id=1, source_target_pairs={{0,1},{1,3},{2,0},{3,2},{4,5},{5,7},{6,4},{7,6},{8,9},{9,11},{10,8... | collective-permute-start | bytes 6291464 | tf_op jit(solution)/shard_map/ppermute | solution.py:338
  4.5 45.4 %collective-permute-start.5 = (bf16[2,32,64,256]{3,2,1,0:T(8,128)(2,1)S(1)}, bf16[2,32,64,256]{3,2,1,0:T(8,128)(2,1)}, u32[]{:S(2)}, u32[]{:S(2)}) collective-permute-start(bf16[2,32,64,256]{3,2,1,0:T(8,128)(2,1)S(1)} %dress.2.refs_0_.refs_4_), channel_id=1, source_target_pairs={{0,12},{3,7},{4,0},{7,11},{8,4},{11,15},{12,8},{15,3},{16,28},{19,... | collective-permute-start | bytes 6291464 | tf_op jit(solution)/shard_map/ppermute | solution.py:338
  44.0 5.9 %collective-permute-start.4 = (bf16[2,32,64,256]{3,2,1,0:T(8,128)(2,1)}, bf16[2,32,64,256]{3,2,1,0:T(8,128)(2,1)}, u32[]{:S(2)}, u32[]{:S(2)}) collective-permute-start(bf16[2,32,64,256]{3,2,1,0:T(8,128)(2,1)} %collective-permute-done.3.refs_4_), channel_id=1, source_target_pairs={{0,1},{3,2},{4,5},{7,6},{8,9},{11,10},{12,13},{15,14},{16,17},{19,... | collective-permute-start | bytes 6291464 | tf_op jit(solution)/shard_map/ppermute | solution.py:338
  46.6 26.4 %collective-permute-start.2 = (bf16[2,32,64,256]{3,2,1,0:T(8,128)(2,1)}, bf16[2,32,64,256]{3,2,1,0:T(8,128)(2,1)}, u32[]{:S(2)}, u32[]{:S(2)}) collective-permute-start(bf16[2,32,64,256]{3,2,1,0:T(8,128)(2,1)} %get-tuple-element.321.refs_1_.refs_5_), channel_id=1, source_target_pairs={{0,1},{1,3},{2,0},{3,2},{4,5},{5,7},{6,4},{7,6},{8,9},{9,11},{10,8... | collective-permute-start | bytes 6291464 | tf_op jit(solution)/shard_map/ppermute | solution.py:338
  46.6 32.2 %collective-permute-start.7 = (bf16[2,32,64,256]{3,2,1,0:T(8,128)(2,1)}, bf16[2,32,64,256]{3,2,1,0:T(8,128)(2,1)}, u32[]{:S(2)}, u32[]{:S(2)}) collective-permute-start(bf16[2,32,64,256]{3,2,1,0:T(8,128)(2,1)} %get-tuple-element.321.refs_1_.refs_5_), channel_id=1, source_target_pairs={{0,12},{3,7},{4,0},{7,11},{8,4},{11,15},{12,8},{15,3},{16,28},{19,... | collective-permute-start | bytes 6291464 | tf_op jit(solution)/shard_map/ppermute | solution.py:338
  72.9 5.9 %collective-permute-start.6 = (bf16[2,32,64,256]{3,2,1,0:T(8,128)(2,1)}, bf16[2,32,64,256]{3,2,1,0:T(8,128)(2,1)}, u32[]{:S(2)}, u32[]{:S(2)}) collective-permute-start(bf16[2,32,64,256]{3,2,1,0:T(8,128)(2,1)} %collective-permute-done.2.refs_5_), channel_id=1, source_target_pairs={{0,1},{3,2},{4,5},{7,6},{8,9},{11,10},{12,13},{15,14},{16,17},{19,... | collective-permute-start | bytes 6291464 | tf_op jit(solution)/shard_map/ppermute | solution.py:338
  75.5 26.4 %collective-permute-start.1 = (bf16[2,32,64,256]{3,2,1,0:T(8,128)(2,1)}, bf16[2,32,64,256]{3,2,1,0:T(8,128)(2,1)}, u32[]{:S(2)}, u32[]{:S(2)}) collective-permute-start(bf16[2,32,64,256]{3,2,1,0:T(8,128)(2,1)} %get-tuple-element.322.refs_2_.refs_6_), channel_id=1, source_target_pairs={{0,1},{1,3},{2,0},{3,2},{4,5},{5,7},{6,4},{7,6},{8,9},{9,11},{10,8... | collective-permute-start | bytes 6291464 | tf_op jit(solution)/shard_map/ppermute | solution.py:338
  75.5 32.3 %collective-permute-start.9 = (bf16[2,32,64,256]{3,2,1,0:T(8,128)(2,1)}, bf16[2,32,64,256]{3,2,1,0:T(8,128)(2,1)}, u32[]{:S(2)}, u32[]{:S(2)}) collective-permute-start(bf16[2,32,64,256]{3,2,1,0:T(8,128)(2,1)} %get-tuple-element.322.refs_2_.refs_6_), channel_id=1, source_target_pairs={{0,12},{3,7},{4,0},{7,11},{8,4},{11,15},{12,8},{15,3},{16,28},{19,... | collective-permute-start | bytes 6291464 | tf_op jit(solution)/shard_map/ppermute | solution.py:338
  101.9 6.0 %collective-permute-start.8 = (bf16[2,32,64,256]{3,2,1,0:T(8,128)(2,1)}, bf16[2,32,64,256]{3,2,1,0:T(8,128)(2,1)}, u32[]{:S(2)}, u32[]{:S(2)}) collective-permute-start(bf16[2,32,64,256]{3,2,1,0:T(8,128)(2,1)} %collective-permute-done.1.refs_6_), channel_id=1, source_target_pairs={{0,1},{3,2},{4,5},{7,6},{8,9},{11,10},{12,13},{15,14},{16,17},{19,... | collective-permute-start | bytes 6291464 | tf_op jit(solution)/shard_map/ppermute | solution.py:338
  104.5 26.4 %collective-permute-start = (bf16[2,32,64,256]{3,2,1,0:T(8,128)(2,1)}, bf16[2,32,64,256]{3,2,1,0:T(8,128)(2,1)}, u32[]{:S(2)}, u32[]{:S(2)}) collective-permute-start(bf16[2,32,64,256]{3,2,1,0:T(8,128)(2,1)} %get-tuple-element.323.refs_3_.refs_7_), channel_id=1, source_target_pairs={{0,1},{1,3},{2,0},{3,2},{4,5},{5,7},{6,4},{7,6},{8,9},{9,11},{10,8... | collective-permute-start | bytes 6291464 | tf_op jit(solution)/shard_map/ppermute | solution.py:338
  104.5 31.6 %collective-permute-start.11 = (bf16[2,32,64,256]{3,2,1,0:T(8,128)(2,1)}, bf16[2,32,64,256]{3,2,1,0:T(8,128)(2,1)}, u32[]{:S(2)}, u32[]{:S(2)}) collective-permute-start(bf16[2,32,64,256]{3,2,1,0:T(8,128)(2,1)} %get-tuple-element.323.refs_3_.refs_7_), channel_id=1, source_target_pairs={{0,12},{3,7},{4,0},{7,11},{8,4},{11,15},{12,8},{15,3},{16,28},{19,... | collective-permute-start | bytes 6291464 | tf_op jit(solution)/shard_map/ppermute | solution.py:338
  130.9 5.4 %collective-permute-start.10 = (bf16[2,32,64,256]{3,2,1,0:T(8,128)(2,1)}, bf16[2,32,64,256]{3,2,1,0:T(8,128)(2,1)}, u32[]{:S(2)}, u32[]{:S(2)}) collective-permute-start(bf16[2,32,64,256]{3,2,1,0:T(8,128)(2,1)} %collective-permute-done.refs_7_), channel_id=1, source_target_pairs={{0,1},{3,2},{4,5},{7,6},{8,9},{11,10},{12,13},{15,14},{16,17},{19,... | collective-permute-start | bytes 6291464 | tf_op jit(solution)/shard_map/ppermute | solution.py:338
  133.5 25.1 %collective-permute-start.14 = (bf16[2,32,64,256]{3,2,1,0:T(8,128)(2,1)}, bf16[2,32,64,256]{3,2,1,0:T(8,128)(2,1)}, u32[]{:S(2)}, u32[]{:S(2)}) collective-permute-start(bf16[2,32,64,256]{3,2,1,0:T(8,128)(2,1)} %broadcast_select_fusion.1), channel_id=1, source_target_pairs={{0,2},{3,1},{4,6},{7,5},{8,10},{11,9},{12,14},{15,13},{16,18},{19,... | collective-permute-start | bytes 6291464 | tf_op jit(solution)/shard_map/ppermute | solution.py:338
  141.8 21.0 %collective-permute-start.15 = (bf16[2,32,64,256]{3,2,1,0:T(8,128)(2,1)}, bf16[2,32,64,256]{3,2,1,0:T(8,128)(2,1)}, u32[]{:S(2)}, u32[]{:S(2)}) collective-permute-start(bf16[2,32,64,256]{3,2,1,0:T(8,128)(2,1)} %collective-permute-done.9), channel_id=1, source_target_pairs={{0,1},{3,2},{4,5},{7,6},{8,9},{11,10},{12,13},{15,14},{16,17},{19,... | collective-permute-start | bytes 6291464 | tf_op jit(solution)/shard_map/ppermute | solution.py:338
  145.4 43.4 %collective-permute-start.12 = (bf16[2,32,64,256]{3,2,1,0:T(8,128)(2,1)}, bf16[2,32,64,256]{3,2,1,0:T(8,128)(2,1)}, u32[]{:S(2)}, u32[]{:S(2)}) collective-permute-start(bf16[2,32,64,256]{3,2,1,0:T(8,128)(2,1)} %broadcast_select_fusion), channel_id=1, source_target_pairs={{0,2},{3,1},{4,6},{7,5},{8,10},{11,9},{12,14},{15,13},{16,18},{19,... | collective-permute-start | bytes 6291464 | tf_op jit(solution)/shard_map/ppermute | solution.py:338
  148.0 36.9 %collective-permute-start.16 = (bf16[2,32,64,256]{3,2,1,0:T(8,128)(2,1)}, bf16[2,32,64,256]{3,2,1,0:T(8,128)(2,1)}, u32[]{:S(2)}, u32[]{:S(2)}) collective-permute-start(bf16[2,32,64,256]{3,2,1,0:T(8,128)(2,1)} %collective-permute-done.5), channel_id=1, source_target_pairs={{0,1},{3,2},{4,5},{7,6},{8,9},{11,10},{12,13},{15,14},{16,17},{19,... | collective-permute-start | bytes 6291464 | tf_op jit(solution)/shard_map/ppermute | solution.py:338
  150.7 38.2 %collective-permute-start.13 = (bf16[2,32,64,256]{3,2,1,0:T(8,128)(2,1)}, bf16[2,32,64,256]{3,2,1,0:T(8,128)(2,1)}, u32[]{:S(2)}, u32[]{:S(2)}) collective-permute-start(bf16[2,32,64,256]{3,2,1,0:T(8,128)(2,1)} %collective-permute-done.11), channel_id=1, source_target_pairs={{0,1},{3,2},{4,5},{7,6},{8,9},{11,10},{12,13},{15,14},{16,17},{19,... | collective-permute-start | bytes 6291464 | tf_op jit(solution)/shard_map/ppermute | solution.py:338
  158.7 30.2 %collective-permute-start.17 = (bf16[2,32,64,256]{3,2,1,0:T(8,128)(2,1)}, bf16[2,32,64,256]{3,2,1,0:T(8,128)(2,1)}, u32[]{:S(2)}, u32[]{:S(2)}) collective-permute-start(bf16[2,32,64,256]{3,2,1,0:T(8,128)(2,1)} %collective-permute-done.7), channel_id=1, source_target_pairs={{0,1},{3,2},{4,5},{7,6},{8,9},{11,10},{12,13},{15,14},{16,17},{19,... | collective-permute-start | bytes 6291464 | tf_op jit(solution)/shard_map/ppermute | solution.py:338
  162.8 34.8 %collective-permute-start.19 = (bf16[2,2,8,64,256]{4,3,2,1,0:T(8,128)(2,1)}, bf16[2,2,8,64,256]{4,3,2,1,0:T(8,128)(2,1)S(1)}, u32[]{:S(2)}, u32[]{:S(2)}) collective-permute-start(bf16[2,2,8,64,256]{4,3,2,1,0:T(8,128)(2,1)} %pick.1), channel_id=1, source_target_pairs={{0,2},{3,1},{4,6},{7,5},{8,10},{11,9},{12,14},{15,13},{16,18},{19,... | collective-permute-start | bytes 3145736 | tf_op jit(solution)/shard_map/ppermute | solution.py:338
  192.8 1.3 collective-permute-start.18
  201.9 2.8 %collective-permute-start.20 = (f32[8,64]{1,0:T(8,128)S(1)}, f32[8,64]{1,0:T(8,128)S(1)}, u32[]{:S(2)}, u32[]{:S(2)}) collective-permute-start(f32[8,64]{1,0:T(8,128)S(1)} %get-tuple-element.354), channel_id=1, source_target_pairs={{0,1},{1,0},{2,3},{3,2},{4,5},{5,4},{6,7},{7,6},{8,9},{9,8},{10,11... | collective-permute-start | bytes 6152 | tf_op jit(solution)/shard_map/ppermute | solution.py:321
  204.7 3.6 %collective-permute-start.21 = (f32[8,64]{1,0:T(8,128)S(1)}, f32[8,64]{1,0:T(8,128)S(1)}, u32[]{:S(2)}, u32[]{:S(2)}) collective-permute-start(f32[8,64]{1,0:T(8,128)S(1)} %add.24), channel_id=1, source_target_pairs={{0,2},{1,3},{2,0},{3,1},{4,6},{5,7},{6,4},{7,5},{8,10},{9,11},{10,... | collective-permute-start | bytes 6152 | tf_op jit(solution)/shard_map/ppermute | solution.py:321
  208.3 3.6 %collective-permute-start.22 = (f32[8,64]{1,0:T(8,128)S(1)}, f32[8,64]{1,0:T(8,128)S(1)}, u32[]{:S(2)}, u32[]{:S(2)}) collective-permute-start(f32[8,64]{1,0:T(8,128)S(1)} %add.25), channel_id=1, source_target_pairs={{0,4},{1,5},{2,6},{3,7},{4,0},{5,1},{6,2},{7,3},{8,12},{9,13},{10,... | collective-permute-start | bytes 6152 | tf_op jit(solution)/shard_map/ppermute | solution.py:321
  211.9 4.5 %collective-permute-start.23 = (f32[8,64]{1,0:T(8,128)S(1)}, f32[8,64]{1,0:T(8,128)S(1)}, u32[]{:S(2)}, u32[]{:S(2)}) collective-permute-start(f32[8,64]{1,0:T(8,128)S(1)} %add.26), channel_id=1, source_target_pairs={{0,8},{1,9},{2,10},{3,11},{4,12},{5,13},{6,14},{7,15},{8,0},{9,1},... | collective-permute-start | bytes 6152 | tf_op jit(solution)/shard_map/ppermute | solution.py:321
  (9 other events, 93.1 us)
where the time goes:
time: 219 us; the launch traced here: 217 us
  Pallas kernels  84.4 us (39%)
  waiting for transfers between devices  68.2 us (31%)
  starting transfers between devices  51.9 us (24%)
  other arithmetic  8.15 us (4%)
  local copies, waits for them, and re-layouts  3.79 us (2%)
    ppermute x20, waiting for transfers between devices, move(): return lax.ppermute(value, 'tm', route)  57.6 us
    ppermute x20, starting transfers between devices, move(): return lax.ppermute(value, 'tm', route)  48 us
    pallas_call x6, Pallas kernels, gram(): pl.pallas_call(functools.partial(gram_kernel, count, left_count), grid=(r...  29.6 us
    pallas_call x4, Pallas kernels, box(): pl.pallas_call(functools.partial(box_kernel, len(left), len(right)), in_s...  25.7 us
    pallas_call x2, Pallas kernels, dress(): pl.pallas_call(dress_kernel, grid=(count * steps,), in_specs=[pl.BlockSpe...  16.3 us
    ppermute x4, waiting for transfers between devices, total_over(): lax.ppermute(value, axis, [(i, i ^ distance) for i in range(devices)])  10.7 us
    pallas_call x2, Pallas kernels, direct(): pl.pallas_call(direct_kernel, in_specs=[smem, smem] + [vmem] * (4 + len(t...  6.92 us
    pallas_call x1, Pallas kernels, pick(): pl.pallas_call(pick_kernel, grid_spec=pltpu.PrefetchScalarGridSpec(num_sc...  5.93 us
  transfers between devices with their start and end apart: 24, of which 9 were waited for; matrix products, arithmetic and copies ran while one was open for 5% of the time, Pallas kernels for 35%

commit v1 on v0

--- a/solution.py
+++ b/solution.py
@@ -7,7 +7,7 @@
 from jax.experimental.pallas import tpu as pltpu
 from jax.sharding import PartitionSpec as P
 
-CHUNKS = 4
+PARTS = (1, 1, 1, 1)
 GROUP = 4
 STEP_ROWS = 16
 STEP_INS = 8
@@ -19,7 +19,7 @@
     return lax.dot_general(left, right, NT, preferred_element_type=jnp.float32)
 
 
-def dress_kernel(fields, factor, *refs):
+def dress_kernel(out_steps, fields, factor, *refs):
     outs, weight = refs[:-1], refs[-1]
     modes = factor.shape[-1]
     step = pl.program_id(0)
@@ -38,37 +38,49 @@
         weight[...],
         preferred_element_type=jnp.float32,
     )
-    steps = pl.num_programs(0) // len(outs)
-    for number, out in enumerate(outs):
-
-        @pl.when(step // steps == number)
+    first = 0
+    for out, count in zip(outs, out_steps):
+
+        @pl.when((step >= first) & (step < first + count))
         def _(out=out):
             out[0] = product[:, :modes].reshape(inserts, rows, modes).astype(out.dtype)
             out[1] = product[:, modes:].reshape(inserts, rows, modes).astype(out.dtype)
 
-
-def dress(fields, factor, first, count):
+        first += count
+
+
+def dress(fields, factor, first, parts):
     inserts, modes = fields.shape[1], fields.shape[-1]
-    rows = modes // CHUNKS
+    rows = modes // sum(PARTS)
     steps = inserts // STEP_INS
     block = (2, STEP_INS, rows, modes)
-
-    def place(number):
-        return lambda g: (0, jnp.clip(g - number * steps, 0, steps - 1), 0, 0)
+    total = sum(parts)
+
+    def place(before, part):
+        def where(g):
+            own = jnp.clip(g - before * steps, 0, part * steps - 1)
+            return 0, own % steps, own // steps, 0
+
+        return where
 
     return pl.pallas_call(
-        dress_kernel,
-        grid=(count * steps,),
+        functools.partial(dress_kernel, [part * steps for part in parts]),
+        grid=(total * steps,),
         in_specs=[
             pl.BlockSpec(block, lambda g: (0, g % steps, first + g // steps, 0)),
             pl.BlockSpec((2, modes, modes), lambda g: (0, 0, 0)),
         ],
-        out_specs=[pl.BlockSpec(block, place(number)) for number in range(count)],
-        out_shape=[jax.ShapeDtypeStruct((2, inserts, rows, modes), fields.dtype)] * count,
+        out_specs=[
+            pl.BlockSpec(block, place(sum(parts[:number]), part))
+            for number, part in enumerate(parts)
+        ],
+        out_shape=[
+            jax.ShapeDtypeStruct((2, inserts, part * rows, modes), fields.dtype) for part in parts
+        ],
         scratch_shapes=[pltpu.VMEM((2 * modes, 2 * modes), fields.dtype)],
         cost_estimate=pl.CostEstimate(
-            flops=16 * count * inserts * rows * modes * modes,
-            bytes_accessed=8 * count * inserts * rows * modes,
+            flops=16 * total * inserts * rows * modes * modes,
+            bytes_accessed=8 * total * inserts * rows * modes,
             transcendentals=0,
         ),
         name="dress",
@@ -92,17 +104,19 @@
         out[...] += product
 
 
-def gram(blocks, left_count, right_count, before):
+def gram(blocks, left_count, right_count, before, offset=0):
     count = len(blocks)
     _, inserts, rows, modes = blocks[0].shape
     size = 2 * inserts
-    spec = pl.BlockSpec((2, inserts, STEP_ROWS, modes), lambda i: (0, 0, i, 0))
+    block = (2, inserts, STEP_ROWS, modes)
+    spec = pl.BlockSpec(block, lambda i: (0, 0, i, 0))
+    last = pl.BlockSpec(block, lambda i: (0, 0, offset // STEP_ROWS + i, 0))
     shape = (left_count * size, right_count * size)
     whole = pl.BlockSpec(shape, lambda i: (0, 0))
     return pl.pallas_call(
         functools.partial(gram_kernel, count, left_count),
         grid=(rows // STEP_ROWS,),
-        in_specs=[spec] * count + [whole],
+        in_specs=[spec] * (count - 1) + [last, whole],
         out_specs=whole,
         out_shape=jax.ShapeDtypeStruct(shape, jnp.float32),
         scratch_shapes=[pltpu.VMEM((count * size, STEP_ROWS * modes), jnp.bfloat16)],
@@ -115,32 +129,41 @@
     )(*blocks, before)
 
 
-def box_kernel(left_count, right_count, ins, entry, coef, weight, before, *refs):
-    left, refs = refs[:left_count], refs[left_count:]
-    right, refs = refs[:right_count], refs[right_count:]
-    extra, (out, held, sems) = refs[:-3], refs[-3:]
-    terms = held.shape[0]
-    rows = left[0].shape[2]
-
-    @pl.loop(0, terms)
-    def _(term):
+def box_kernel(counts, ins, scale, before, *refs):
+    groups = []
+    for left_count, right_count, extra_count in counts:
+        left, refs = refs[:left_count], refs[left_count:]
+        right, refs = refs[:right_count], refs[right_count:]
+        extra, refs = refs[:extra_count], refs[extra_count:]
+        groups.append((left, right, extra))
+    out, held, sems = refs
+    terms = held.shape[0] // len(groups)
+
+    def fetch(group, term):
+        left, right, extra = groups[group]
+        slot = group * terms + term
         for place in range(4):
-            where = ins[place, term]
+            where = ins[place, slot]
             sources = [ref.at[:, where] for ref in (right if place % 2 else left)]
             if place % 2 == 0:
                 for ref in extra:
                     where = (place // 2) * terms + term
                     sources += [ref.at[number, :, where] for number in range(ref.shape[0])]
-            for number, source in enumerate(sources):
+            start = 0
+            for source in sources:
+                rows = source.shape[1]
                 pltpu.make_async_copy(
-                    source,
-                    held.at[term, place, :, pl.ds(number * rows, rows)],
-                    sems.at[term],
+                    source, held.at[slot, place, :, pl.ds(start, rows)], sems.at[slot]
                 ).start()
-
-    def product(term, one, other):
-        real, imag = held[term, one, 0], held[term, one, 1]
-        other_side = jnp.concatenate([held[term, other, 0], held[term, other, 1]], axis=1)
+                start += rows
+
+    @pl.loop(0, terms)
+    def _(term):
+        fetch(0, term)
+
+    def product(slot, one, other):
+        real, imag = held[slot, one, 0], held[slot, one, 1]
+        other_side = jnp.concatenate([held[slot, other, 0], held[slot, other, 1]], axis=1)
         return (
             nt_dot(jnp.concatenate([real, imag], axis=1), other_side),
             nt_dot(jnp.concatenate([imag, -real], axis=1), other_side),
@@ -149,78 +172,106 @@
     out[...] = before[...]
     spot = lax.broadcasted_iota(jnp.int32, out.shape, 1)
     line = lax.broadcasted_iota(jnp.int32, out.shape, 0)
-
-    @pl.loop(0, terms)
-    def _(term):
-        pltpu.make_async_copy(held.at[term], held.at[term], sems.at[term]).wait()
-        first_real, first_imag = product(term, 0, 1)
-        second_real, second_imag = product(term, 3, 2)
-        real = jnp.sum(first_real * second_real + first_imag * second_imag) * coef[term]
-        imag = jnp.sum(first_imag * second_real - first_real * second_imag) * coef[term]
-        imag = imag * weight[3]
-        added = jnp.zeros(out.shape, jnp.float32)
-        for apart in range(3):
-            added = jnp.where(line == 2 * apart, real * weight[apart], added)
-            added = jnp.where(line == 2 * apart + 1, imag * weight[apart], added)
-        out[...] -= jnp.where(spot == entry[term], added, 0.0)
-
-
-def box(left, right, ins, entry, coef, weight, before, extra=None):
-    extra = [] if extra is None else [extra]
-    terms = ins.shape[1]
-    modes = left[0].shape[3]
-    count = len(left) + len(right) + len(extra)
+    for group in range(len(groups)):
+
+        @pl.loop(0, terms)
+        def _(term, group=group):
+            if group + 1 < len(groups):
+                fetch(group + 1, term)
+            slot = group * terms + term
+            pltpu.make_async_copy(held.at[slot], held.at[slot], sems.at[slot]).wait()
+            first_real, first_imag = product(slot, 0, 1)
+            second_real, second_imag = product(slot, 3, 2)
+            real = jnp.sum(first_real * second_real + first_imag * second_imag)
+            imag = jnp.sum(first_imag * second_real - first_real * second_imag)
+            imag = imag * scale[3, slot]
+            added = jnp.zeros(out.shape, jnp.float32)
+            for apart in range(3):
+                added = jnp.where(line == 2 * apart, real * scale[apart, slot], added)
+                added = jnp.where(line == 2 * apart + 1, imag * scale[apart, slot], added)
+            out[...] -= jnp.where(spot == ins[4, slot], added, 0.0)
+
+
+def box(groups, table, before):
+    ins, scale = table
+    slots = ins.shape[1]
+    modes = groups[0][0][0].shape[3]
+    kind = groups[0][0][0].dtype
+    arrays = [ref for group in groups for refs in group for ref in refs]
     smem = pl.BlockSpec(memory_space=pltpu.SMEM)
     vmem = pl.BlockSpec(memory_space=pltpu.VMEM)
     return pl.pallas_call(
-        functools.partial(box_kernel, len(left), len(right)),
-        in_specs=[smem] * 4 + [vmem] + [pl.BlockSpec(memory_space=pl.ANY)] * count,
+        functools.partial(box_kernel, [tuple(len(refs) for refs in group) for group in groups]),
+        in_specs=[smem, smem, vmem] + [pl.BlockSpec(memory_space=pl.ANY)] * len(arrays),
         out_specs=vmem,
         out_shape=jax.ShapeDtypeStruct(before.shape, jnp.float32),
         scratch_shapes=[
-            pltpu.VMEM((terms, 4, 2, modes, modes), left[0].dtype),
-            pltpu.SemaphoreType.DMA((terms,)),
+            pltpu.VMEM((slots, 4, 2, modes, modes), kind),
+            pltpu.SemaphoreType.DMA((slots,)),
         ],
         cost_estimate=pl.CostEstimate(
-            flops=32 * terms * modes * modes * modes,
-            bytes_accessed=16 * terms * modes * modes,
+            flops=32 * slots * modes * modes * modes,
+            bytes_accessed=16 * slots * modes * modes,
             transcendentals=0,
         ),
         name="box",
-    )(ins, entry, coef, weight, before, *left, *right, *extra)
-
-
-def pick_kernel(upper, ins, *refs):
-    del ins
-    blocks, out = refs[:-1], refs[-1]
-    half = len(blocks) // 2
-
-    @pl.when(upper[0] == 1)
-    def _():
-        for number in range(half):
-            out[number] = blocks[half + number][...]
-
-    @pl.when(upper[0] == 0)
-    def _():
-        for number in range(half):
-            out[number] = blocks[number][...]
-
-
-def pick(blocks, places, upper):
-    _, _, rows, modes = blocks[0].shape
-    half, count = len(blocks) // 2, places.shape[0]
-    spec = pl.BlockSpec((2, 1, rows, modes), lambda l, upper, ins: (0, ins[l], 0, 0))
+    )(ins, scale, before, *arrays)
+
+
+def pick_kernel(count, upper, places, *refs):
+    blocks, outs, (held, sems) = refs[:count], refs[count:-2], refs[-2:]
+    terms = places.shape[0]
+
+    def fetch(term):
+        def go(sources, start=0):
+            for source in sources:
+                pltpu.make_async_copy(
+                    source, held.at[term, :, pl.ds(start, source.shape[1])], sems.at[term]
+                ).start()
+                start += source.shape[1]
+
+        where = places[term]
+
+        @pl.when(upper[0] == 1)
+        def _():
+            go([ref.at[:, where] for ref in blocks[count // 2 :]])
+
+        @pl.when(upper[0] == 0)
+        def _():
+            go([ref.at[:, where] for ref in blocks[: count // 2]])
+
+    for term in range(terms):
+        fetch(term)
+    share = terms // len(outs)
+    for term in range(terms):
+        pltpu.make_async_copy(held.at[term], held.at[term], sems.at[term]).wait()
+        target = outs[term // share].at[0, :, term % share]
+        pltpu.make_async_copy(held.at[term], target, sems.at[term]).start()
+    for term in range(terms):
+        target = outs[term // share].at[0, :, term % share]
+        pltpu.make_async_copy(held.at[term], target, sems.at[term]).wait()
+
+
+def pick(blocks, places, upper, shares):
+    modes = blocks[0].shape[3]
+    rows = modes // 2
+    count = places.shape[0]
+    smem = pl.BlockSpec(memory_space=pltpu.SMEM)
+    hbm = pl.BlockSpec(memory_space=pl.ANY)
     return pl.pallas_call(
-        pick_kernel,
-        grid_spec=pltpu.PrefetchScalarGridSpec(
-            num_scalar_prefetch=2,
-            grid=(count,),
-            in_specs=[spec] * len(blocks),
-            out_specs=pl.BlockSpec(
-                (half, 2, 1, rows, modes), lambda l, upper, ins: (0, 0, l, 0, 0)
-            ),
+        functools.partial(pick_kernel, len(blocks)),
+        in_specs=[smem, smem] + [hbm] * len(blocks),
+        out_specs=[hbm] * shares,
+        out_shape=[
+            jax.ShapeDtypeStruct((1, 2, count // shares, rows, modes), blocks[0].dtype)
+        ] * shares,
+        scratch_shapes=[
+            pltpu.VMEM((count, 2, rows, modes), blocks[0].dtype),
+            pltpu.SemaphoreType.DMA((count,)),
+        ],
+        cost_estimate=pl.CostEstimate(
+            flops=0, bytes_accessed=8 * count * rows * modes, transcendentals=0
         ),
-        out_shape=jax.ShapeDtypeStruct((half, 2, count, rows, modes), blocks[0].dtype),
         name="pick",
     )(upper, places, *blocks)
 
@@ -345,8 +396,10 @@
 
     fields = meson_fields[:, :, 0]
     factor = perambulators[:, 0]
-    own = dress(fields, factor, 0, 1) + dress(fields, factor, 1, CHUNKS - 1)
-    half = CHUNKS // 2
+    own = dress(fields, factor, 0, PARTS[:1])
+    own = own + dress(fields, after(factor, own[0]), PARTS[0], PARTS[1:])
+    count = len(own)
+    half = count // 2
 
     across = {0: lambda i: i + 1, 1: lambda i: i + 2, 2: lambda i: i - 2, 3: lambda i: i - 1}
     along = {0: lambda i: i - GROUP, 3: lambda i: i + GROUP}
@@ -363,16 +416,25 @@
     late_coef = jnp.where(role == 1, box_coef[part:], box_coef[:part])
 
     near, far = [], []
-    for chunk in range(CHUNKS):
+    for chunk in range(count):
         near.append(move(own[chunk], across))
         far.append(move(own[chunk], along))
-    split = [jnp.where(role == 0, own[half + j], own[j]) for j in range(half)]
-    chosen = jnp.concatenate([send_table[0], send_table[2]])
-    extra = pick(own, chosen, jnp.where(role == 0, 0, 1).astype(jnp.int32)[None])
-    split_in = []
-    for piece in split:
-        split_in.append(move(after(piece, near[CHUNKS - 2]), cross))
-    extra_in = move(after(extra, near[CHUNKS - 2]), cross)
+    rows = own[0].shape[2]
+    cuts = [(j, 0, rows) for j in range(half - 1)]
+    cuts += [(half - 1, 0, rows // 2), (half - 1, rows // 2, rows // 2)]
+    split = [
+        jnp.where(
+            role == 0,
+            own[half + j][:, :, start : start + length],
+            own[j][:, :, start : start + length],
+        )
+        for j, start, length in cuts
+    ]
+    upper = jnp.where(role == 0, 0, 1).astype(jnp.int32)[None]
+    shares = [slice(0, part // 2), slice(part // 2, part)]
+    chosen = [send_table[row, share] for share in shares for row in (0, 2)]
+    extra = pick(own, jnp.concatenate(chosen), upper, len(shares))
+    mate = move(after(own[-1], extra[0]), beside)
 
     edge = (role == 0) | (role == 3)
     one, zero = jnp.float32(1.0), jnp.float32(0.0)
@@ -380,11 +442,16 @@
     def weights(first, second, third):
         return jnp.stack([first + zero, second + zero, third + zero])
 
-    def with_sign(weight, swap):
-        return jnp.concatenate([weight, jnp.where(swap == 1, -one, one)[None]])
+    def box_table(table, entry, coef, weight, swap):
+        scale = [weight[apart] * coef for apart in range(3)]
+        scale.append(jnp.where(swap == 1, -one, one) * jnp.ones_like(coef))
+        return jnp.concatenate([table, entry[None]]), jnp.stack(scale)
 
     def role_table(swap):
         return jnp.where(swap == 1, swapped_table, ins_table)
+
+    def join(first, second):
+        return tuple(jnp.concatenate([a, b], axis=1) for a, b in zip(first, second))
 
     outer = jnp.where(edge, one, zero)
     inner = one - outer
@@ -396,15 +463,40 @@
     near_swap = by_role(0, 1, 0, 1)
     third_swap = by_role(0, 0, 1, 1)
     size = 2 * fields.shape[1]
-
-    total = box(
-        own, own, ins_table, box_entry, box_coef, with_sign(same_weight, 0),
-        jnp.zeros((8, entries), jnp.float32),
+    with_entry = functools.partial(box_table, entry=box_entry, coef=box_coef)
+    same_table = with_entry(ins_table, weight=same_weight, swap=0)
+    near_table = with_entry(role_table(near_swap), weight=near_weight, swap=near_swap)
+    third_table = with_entry(role_table(third_swap), weight=third_weight, swap=third_swap)
+    both_table = join(near_table, third_table)
+    late_swap = by_role(0, 0, 1, 0)
+    late_tables = [
+        box_table(late_table[:, share], late_entry[share], late_coef[share], both_inner, late_swap)
+        for share in shares
+    ]
+    main_scalars = (
+        jnp.stack([jnp.int32(0), near_swap, third_swap, edge.astype(jnp.int32)]),
+        jnp.concatenate([same_weight, near_weight, third_weight]),
     )
+    split_scalars = (jnp.zeros((4,), jnp.int32), split_weight)
+    direct_terms = (direct_ins.T, direct_coef[None], direct_entry[None])
+    small = (
+        near_table, third_table, both_table, late_tables, main_scalars, split_scalars, direct_terms
+    )
+
+    total = box([(own, own, [])], same_table, jnp.zeros((8, entries), jnp.float32))
     table = jnp.zeros((2 * size, 3 * size), jnp.float32)
-    early = (total, extra) + tuple(split)
-    near_beside = []
-    for chunk in range(CHUNKS):
+    (total, small, extra, split), _ = lax.optimization_barrier(((total, small, extra, split), near[0]))
+    near_table, third_table, both_table, late_tables, main_scalars, split_scalars, direct_terms = small
+    split_in, extra_in = [], []
+    for piece in split:
+        split_in.append(move(after(piece, near[-2]), cross))
+    for piece in extra:
+        extra_in.append(move(after(piece, near[-2]), cross))
+    early = (total,)
+    near_beside, far_beside = [], []
+    for chunk in range(count):
+        if chunk < count - 1:
+            far_beside.append(move(after(far[chunk], *early), beside))
         near_beside.append(move(after(near[chunk], *early), beside))
         table = lax.cond(
             edge,
@@ -413,46 +505,41 @@
             own[chunk], near[chunk], far[chunk], near_beside[chunk], table,
         )
         early = (table,)
-    far_beside = [move(after(piece, table), beside) for piece in far]
-    total = after(total, table)
-    total = box(
-        own, near, role_table(near_swap), box_entry, box_coef,
-        with_sign(near_weight, near_swap), total,
-    )
+        if chunk == count - 2:
+            total = lax.cond(
+                edge,
+                lambda o, m, k, t: t,
+                lambda o, m, k, t: box([(o, m, [])], k, t),
+                own, near[:-1] + [mate], near_table, after(total, table),
+            )
+            early = (table, total)
+    far_beside.append(move(after(far[-1], table), beside))
     total = lax.cond(
         edge,
-        lambda o, a, z, c, *rest: box(a, z, *rest),
-        lambda o, a, z, c, *rest: box(o, c, *rest),
-        own, near, far, near_beside, role_table(third_swap), box_entry, box_coef,
-        with_sign(third_weight, third_swap), total,
+        lambda o, a, z, c, k, j, t: box([(o, a, []), (a, z, [])], j, t),
+        lambda o, a, z, c, k, j, t: box([(o, c, [])], k, t),
+        own, near, far, near_beside, third_table, both_table, after(total, table),
     )
-    direct_table = direct_ins.T
-    total = direct(
-        [table], 3,
-        jnp.stack([jnp.int32(0), near_swap, third_swap, edge.astype(jnp.int32)]),
-        jnp.concatenate([same_weight, near_weight, third_weight]),
-        direct_table, direct_coef[None], direct_entry[None], total,
-    )
+    total = direct([table], 3, *main_scalars, *direct_terms, total)
     split_gram = after(jnp.zeros((size, size), jnp.float32), total)
-    for j in range(half):
+    for piece, (j, start, _) in zip(split_in, cuts):
         split_gram = lax.cond(
             role == 1,
-            lambda v, lo, hi, t: gram([v, lo], 1, 1, t),
-            lambda v, lo, hi, t: gram([v, hi], 1, 1, t),
-            split_in[j], far_beside[j], far_beside[half + j], split_gram,
+            lambda v, lo, hi, t, start=start: gram([v, lo], 1, 1, t, start),
+            lambda v, lo, hi, t, start=start: gram([v, hi], 1, 1, t, start),
+            piece, far_beside[j], far_beside[half + j], split_gram,
         )
     split_other = move(split_gram, {2: lambda i: i - 5})
-    total = direct(
-        [split_gram, split_other], 1, jnp.zeros((4,), jnp.int32), split_weight,
-        direct_table, direct_coef[None], direct_entry[None], total,
-    )
-    total = lax.cond(
-        role == 1,
-        lambda v, x, f, *rest: box(v, f, *rest, extra=x),
-        lambda v, x, f, *rest: box(v, f[half:] + f[:half], *rest, extra=x),
-        split_in, extra_in, far_beside, late_table, late_entry, late_coef,
-        with_sign(both_inner, by_role(0, 0, 1, 0)), total,
-    )
+    total = after(total, split_gram)
+    for number in range(len(shares)):
+        total = lax.cond(
+            role == 1,
+            lambda v, x, f, k, t: box([(v, f, [x])], k, t),
+            lambda v, x, f, k, t: box([(v, f[half:] + f[:half], [x])], k, t),
+            split_in, extra_in[number], far_beside, late_tables[number], total,
+        )
+        if number == 0:
+            total = direct([split_gram, split_other], 1, *split_scalars, *direct_terms, total)
     summed = total_over(total, "tm") / devices
     mine = lax.dynamic_slice_in_dim(summed[:6], here * owned, owned, axis=1)
     return mine.reshape(3, 2, owned)

time: 219 us -> 234 us (1.068)
  waiting for transfers between devices: 68.2 us -> 79.7 us
  starting transfers between devices: 51.9 us -> 56.5 us
  Pallas kernels: 84.4 us -> 80.7 us
    ppermute x20 -> x23, waiting for transfers between devices: 57.6 us -> 67.5 us  [move(): return lax.ppermute(value, 'tm', route)]
    ppermute x20 -> x23, starting transfers between devices: 48 us -> 55.7 us  [move(): return lax.ppermute(value, 'tm', route)]
    pallas_call x7, Pallas kernels: 47.9 us -> 44.5 us  [the longest x4 25.5 us: box(): pl.pallas_call(functools.partial(box_kernel, [tuple((len(refs) for refs i...]
    ppermute x4, starting transfers between devices: 3.91 us -> 0.76 us  [total_over(): lax.ppermute(value, axis, [(i, i ^ distance) for i in range(devices)])]
    pallas_call x6 -> x7, Pallas kernels: 29.6 us -> 29.9 us  [gram(): pl.pallas_call(functools.partial(gram_kernel, count, left_count), grid=(r...]
  transfers between devices with their start and end apart: 24 -> 27, of which waited for: 9 -> 8; matrix products, arithmetic and copies ran while one was open for 5% -> 6% of each run, Pallas kernels for 35% -> 32%
where the time goes in v1:
time: 234 us; the launch traced here: 233 us
  Pallas kernels  80.7 us (34%)
  waiting for transfers between devices  79.7 us (34%)
  starting transfers between devices  56.5 us (24%)
  other arithmetic  9.23 us (4%)
  local copies, waits for them, and re-layouts  5.81 us (2%)
    ppermute x23, waiting for transfers between devices, move(): return lax.ppermute(value, 'tm', route)  67.5 us
    ppermute x23, starting transfers between devices, move(): return lax.ppermute(value, 'tm', route)  55.7 us
    pallas_call x7, Pallas kernels, gram(): pl.pallas_call(functools.partial(gram_kernel, count, left_count), grid=(r...  29.9 us
    pallas_call x4, Pallas kernels, box(): pl.pallas_call(functools.partial(box_kernel, [tuple((len(refs) for refs i...  25.5 us
    pallas_call x2, Pallas kernels, dress(): pl.pallas_call(functools.partial(dress_kernel, [part * steps for part in...  16.4 us
    ppermute x4, waiting for transfers between devices, total_over(): lax.ppermute(value, axis, [(i, i ^ distance) for i in range(devices)])  12.2 us
    pallas_call x2, Pallas kernels, direct(): pl.pallas_call(direct_kernel, in_specs=[smem, smem] + [vmem] * (4 + len(t...  6.31 us
    select_n x2, other arithmetic, local(): jnp.where(role == 0, own[half + j][:, :, start:start + length], own[j][:,...  5.44 us
  transfers between devices with their start and end apart: 27, of which 8 were waited for; matrix products, arithmetic and copies ran while one was open for 6% of the time, Pallas kernels for 32%

profile of v1, /device:TPU:0, one launch (start us, length us, event | category | flops | bytes accessed | tf_op | source)
XLA Modules:
  0.0 232.7 jit_solution(2799973535192243118)
XLA Ops:
  0.0 4.0 %dress.2.refs_0_.refs_4_ = bf16[2,32,64,256]{3,2,1,0:T(8,128)(2,1)S(1)} custom-call(bf16[2,32,256,256]{3,2,1,0:T(8,128)(2,1)} %bitcast.49, bf16[2,256,256]{2,1,0:T(8,128)(2,1)} %bitcast.51), custom_call_target="tpu_custom_call" | custom-call | flops 2147483648 | bytes 4194304 | tf_op jit(solution)/shard_map/dress/pallas_call | solution.py:66
  4.5 6.5 %collective-permute-start.4 = (bf16[2,32,64,256]{3,2,1,0:T(8,128)(2,1)S(1)}, bf16[2,32,64,256]{3,2,1,0:T(8,128)(2,1)}, u32[]{:S(2)}, u32[]{:S(2)}) collective-permute-start(bf16[2,32,64,256]{3,2,1,0:T(8,128)(2,1)S(1)} %dress.2.refs_0_.refs_4_), channel_id=1, source_target_pairs={{0,12},{3,7},{4,0},{7,11},{8,4},{11,15},{12,8},{15,3},{16,28},{19,... | collective-permute-start | bytes 6291464 | tf_op jit(solution)/shard_map/ppermute | solution.py:389
  12.6 12.4 %dress.3 = (bf16[2,32,64,256]{3,2,1,0:T(8,128)(2,1)}, bf16[2,32,64,256]{3,2,1,0:T(8,128)(2,1)}, bf16[2,32,64,256]{3,2,1,0:T(8,128)(2,1)}) custom-call(bf16[2,32,256,256]{3,2,1,0:T(8,128)(2,1)} %bitcast.50, bf16[2,256,256]{2,1,0:T(8,128)(2,1)} %bitcast.52), custom_call_target="tpu_custom_call" | custom-call | flops 6442450944 | bytes 12582912 | tf_op jit(solution)/shard_map/dress/pallas_call | solution.py:66
  31.9 3.9 %slice_select_fusion = (bf16[2,32,32,256]{3,2,1,0:T(8,128)(2,1)}, bf16[2,32,32,256]{3,2,1,0:T(8,128)(2,1)}) fusion(bf16[2,32,64,256]{3,2,1,0:T(8,128)(2,1)} %get-tuple-element.474.refs_1_.refs_5_, bf16[2,32,64,256]{3,2,1,0:T(8,128)(2,1)} %get-tuple-element.499.refs_3_.refs_7_, pred[]{:T(512)S(6)} %eq.18), kind=kLoop, calls=%fused_computation.2 | loop fusion | flops 1048576 | bytes 6291457 | tf_op jit(solution)/shard_map/jit(_where)/select_n | solution.py:426
  37.9 7.3 %box.15 = f32[8,64]{1,0:T(8,128)S(1)} custom-call(s32[5,8]{1,0:T(8,128)} %get-tuple-element.593.ins, f32[4,8]{1,0:T(4,128)} %get-tuple-element.586.scale, f32[8,64]{1,0:T(8,128)} %broadcast_in_dim.36.before, bf16[2,32,64,256]{3,2,1,0:T(8,128)(2,1)S(1)} %dress.2.refs_0_.refs_4_, bf16[2,32,64,256]{3,2,1,0:T(8,128)(2,1)} %get-tuple-element.474.refs_1_.refs_5_, ...), custom_call_target="tpu_custom_call" | custom-call | flops 4294967296 | bytes 8388608 | tf_op jit(solution)/shard_map/box/pallas_call | solution.py:203
  51.5 5.9 %conditional.11 = (f32[128,192]{1,0:T(8,128)S(1)}) conditional(s32[]{:T(128)} %convert_element_type.5, (bf16[2,32,64,256]{3,2,1,0:T(8,128)(2,1)S(1)}, bf16[2,32,64,256]{3,2,1,0:T(8,128)(2,1)}, bf16[2,32,64,256]{3,2,1,0:T(8,128)(2,1)}) %tuple.94, (bf16[2,32,64,256]{3,2,1,0:T(8,128)(2,1)S(1)}, bf16[2,32,64,256]{3,2,1,0:T(8,128)(2,1)}, ...), branch_computations={%region_0.1_spmd, %region_1.2_spmd} | conditional | flops 6442450944 | bytes 6389772 | solution.py:501
  52.1 5.3 %gram.15 = f32[128,192]{1,0:T(8,128)S(1)} custom-call(bf16[2,32,64,256]{3,2,1,0:T(8,128)(2,1)S(1)} %get-tuple-element.286.refs_0_, bf16[2,32,64,256]{3,2,1,0:T(8,128)(2,1)} %get-tuple-element.287.refs_1_, bf16[2,32,64,256]{3,2,1,0:T(8,128)(2,1)} %get-tuple-element.288.refs_2_, f32[128,192]{1,0:T(8,128)} %broadcast_in_dim.10.refs_3_), custom_call_target="tpu_custom_call" | custom-call | flops 6442450944 | bytes 6291456 | tf_op jit(solution)/shard_map/cond/branch_1_fun/gram/pallas_call | solution.py:116
  57.4 16.8 %collective-permute-done.2 = bf16[2,32,64,256]{3,2,1,0:T(8,128)(2,1)} collective-permute-done((bf16[2,32,64,256]{3,2,1,0:T(8,128)(2,1)}, bf16[2,32,64,256]{3,2,1,0:T(8,128)(2,1)}, u32[]{:S(2)}, u32[]{:S(2)}) %collective-permute-start.2) | collective-permute-done | bytes 2097184 | tf_op jit(solution)/shard_map/ppermute | solution.py:389
  80.4 5.5 %conditional.12 = (f32[128,192]{1,0:T(8,128)S(1)}) conditional(s32[]{:T(128)} %convert_element_type.5, (bf16[2,32,64,256]{3,2,1,0:T(8,128)(2,1)}, bf16[2,32,64,256]{3,2,1,0:T(8,128)(2,1)}, bf16[2,32,64,256]{3,2,1,0:T(8,128)(2,1)}, f32[128,192]{1,0:T(8,128)S(1)}) %tuple.97, (bf16[2,32,64,256]{3,2,1,0:T(8,128)(2,1)}, ...), branch_computations={%region_2.3_spmd, %region_3.4_spmd} | conditional | flops 6442450944 | bytes 6291464 | solution.py:501
  80.4 5.5 %gram.17 = f32[128,192]{1,0:T(8,128)S(1)} custom-call(bf16[2,32,64,256]{3,2,1,0:T(8,128)(2,1)} %get-tuple-element.307.refs_0_, bf16[2,32,64,256]{3,2,1,0:T(8,128)(2,1)} %get-tuple-element.308.refs_1_, bf16[2,32,64,256]{3,2,1,0:T(8,128)(2,1)} %get-tuple-element.309.refs_2_, f32[128,192]{1,0:T(8,128)S(1)} %get-tuple-element.310.refs_3_), custom_call_target="tpu_custom_call" | custom-call | flops 6442450944 | bytes 6291456 | tf_op jit(solution)/shard_map/cond/branch_1_fun/gram/pallas_call | solution.py:116
  85.9 17.2 %collective-permute-done.1 = bf16[2,32,64,256]{3,2,1,0:T(8,128)(2,1)} collective-permute-done((bf16[2,32,64,256]{3,2,1,0:T(8,128)(2,1)}, bf16[2,32,64,256]{3,2,1,0:T(8,128)(2,1)}, u32[]{:S(2)}, u32[]{:S(2)}) %collective-permute-start.1) | collective-permute-done | bytes 2097184 | tf_op jit(solution)/shard_map/ppermute | solution.py:389
  112.1 5.5 %conditional.13 = (f32[128,192]{1,0:T(8,128)S(1)}) conditional(s32[]{:T(128)} %convert_element_type.5, (bf16[2,32,64,256]{3,2,1,0:T(8,128)(2,1)}, bf16[2,32,64,256]{3,2,1,0:T(8,128)(2,1)}, bf16[2,32,64,256]{3,2,1,0:T(8,128)(2,1)}, f32[128,192]{1,0:T(8,128)S(1)}) %tuple.100, (bf16[2,32,64,256]{3,2,1,0:T(8,128)(2,1)}, ...), branch_computations={%region_4.5_spmd, %region_5.6_spmd} | conditional | flops 6442450944 | bytes 6291464 | solution.py:501
  112.1 5.5 %gram.19 = f32[128,192]{1,0:T(8,128)S(1)} custom-call(bf16[2,32,64,256]{3,2,1,0:T(8,128)(2,1)} %get-tuple-element.315.refs_0_, bf16[2,32,64,256]{3,2,1,0:T(8,128)(2,1)} %get-tuple-element.316.refs_1_, bf16[2,32,64,256]{3,2,1,0:T(8,128)(2,1)} %get-tuple-element.317.refs_2_, f32[128,192]{1,0:T(8,128)S(1)} %get-tuple-element.318.refs_3_), custom_call_target="tpu_custom_call" | custom-call | flops 6442450944 | bytes 6291456 | tf_op jit(solution)/shard_map/cond/branch_1_fun/gram/pallas_call | solution.py:116
  117.7 17.1 %collective-permute-done.10 = bf16[2,32,64,256]{3,2,1,0:T(8,128)(2,1)} collective-permute-done((bf16[2,32,64,256]{3,2,1,0:T(8,128)(2,1)}, bf16[2,32,64,256]{3,2,1,0:T(8,128)(2,1)}, u32[]{:S(2)}, u32[]{:S(2)}) %collective-permute-start.10) | collective-permute-done | bytes 2097184 | tf_op jit(solution)/shard_map/ppermute | solution.py:389
  149.3 5.5 %conditional.15 = (f32[128,192]{1,0:T(8,128)S(1)}) conditional(s32[]{:T(128)} %convert_element_type.5, (bf16[2,32,64,256]{3,2,1,0:T(8,128)(2,1)}, bf16[2,32,64,256]{3,2,1,0:T(8,128)(2,1)}, bf16[2,32,64,256]{3,2,1,0:T(8,128)(2,1)}, f32[128,192]{1,0:T(8,128)S(1)}) %tuple.106, (bf16[2,32,64,256]{3,2,1,0:T(8,128)(2,1)}, ...), branch_computations={%region_8.9_spmd, %region_9.10_spmd} | conditional | flops 6442450944 | bytes 6291464 | solution.py:501
  149.3 5.5 %gram.21 = f32[128,192]{1,0:T(8,128)S(1)} custom-call(bf16[2,32,64,256]{3,2,1,0:T(8,128)(2,1)} %get-tuple-element.334.refs_0_, bf16[2,32,64,256]{3,2,1,0:T(8,128)(2,1)} %get-tuple-element.335.refs_1_, bf16[2,32,64,256]{3,2,1,0:T(8,128)(2,1)} %get-tuple-element.336.refs_2_, f32[128,192]{1,0:T(8,128)S(1)} %get-tuple-element.337.refs_3_), custom_call_target="tpu_custom_call" | custom-call | flops 6442450944 | bytes 6291456 | tf_op jit(solution)/shard_map/cond/branch_1_fun/gram/pallas_call | solution.py:116
  157.5 16.3 %collective-permute-done.16 = bf16[2,32,64,256]{3,2,1,0:T(8,128)(2,1)} collective-permute-done((bf16[2,32,64,256]{3,2,1,0:T(8,128)(2,1)}, bf16[2,32,64,256]{3,2,1,0:T(8,128)(2,1)}, u32[]{:S(2)}, u32[]{:S(2)}) %collective-permute-start.16) | collective-permute-done | bytes 2097184 | tf_op jit(solution)/shard_map/ppermute | solution.py:389
  173.8 5.4 %collective-permute-start.13 = (bf16[2,32,32,256]{3,2,1,0:T(8,128)(2,1)}, bf16[2,32,32,256]{3,2,1,0:T(8,128)(2,1)}, u32[]{:S(2)}, u32[]{:S(2)}) collective-permute-start(bf16[2,32,32,256]{3,2,1,0:T(8,128)(2,1)} %get-tuple-element.505), channel_id=1, source_target_pairs={{0,2},{3,1},{4,6},{7,5},{8,10},{11,9},{12,14},{15,13},{16,18},{19,... | collective-permute-start | bytes 3145736 | tf_op jit(solution)/shard_map/ppermute | solution.py:389
  183.4 12.0 %conditional.16 = (f32[8,64]{1,0:T(8,128)S(1)}) conditional(s32[]{:T(128)} %convert_element_type.5, (s32[5,8]{1,0:T(8,128)S(1)}, f32[4,8]{1,0:T(4,128)S(1)}, f32[8,64]{1,0:T(8,128)S(1)}, bf16[2,32,64,256]{3,2,1,0:T(8,128)(2,1)S(1)}, bf16[2,32,64,256]{3,2,1,0:T(8,128)(2,1)}, /*index=5*/bf16[2,32,64,256]{3,2,1,0:T(8,128)(2,1)}, ...), branch_computations={%region_10.11_spmd, %region_11.12_spmd} | conditional | flops 8589934592 | bytes 16777224 | solution.py:517
  183.4 11.8 %box.10 = f32[8,64]{1,0:T(8,128)S(1)} custom-call(s32[5,16]{1,0:T(8,128)S(1)} %get-tuple-element.349.ins, f32[4,16]{1,0:T(4,128)S(1)} %get-tuple-element.350.scale, f32[8,64]{1,0:T(8,128)S(1)} %get-tuple-element.351.before, bf16[2,32,64,256]{3,2,1,0:T(8,128)(2,1)S(1)} %get-tuple-element.352.refs_0_, bf16[2,32,64,256]{3,2,1,0:T(8,128)(2,1)} %get-tuple-element.353.refs_1_, ...), custom_call_target="tpu_custom_call" | custom-call | flops 8589934592 | bytes 16777216 | tf_op jit(solution)/shard_map/cond/branch_1_fun/box/pallas_call | solution.py:203
  198.9 3.9 %conditional.17 = (f32[64,64]{1,0:T(8,128)S(1)}) conditional(s32[]{:T(128)} %convert_element_type.4, (bf16[2,32,64,256]{3,2,1,0:T(8,128)(2,1)}, bf16[2,32,64,256]{3,2,1,0:T(8,128)(2,1)}, f32[64,64]{1,0:T(8,128)S(1)}) %tuple.117, (bf16[2,32,64,256]{3,2,1,0:T(8,128)(2,1)}, bf16[2,32,64,256]{3,2,1,0:T(8,128)(2,1)}, f32[64,64]{1,0:T(8,128)S(1)}) %tuple.119), branch_computations={%region_12.13_spmd, %region_13.14_spmd} | conditional | flops 1073741824 | bytes 4194312 | solution.py:526
  198.9 3.9 %gram.22 = f32[64,64]{1,0:T(8,128)S(1)} custom-call(bf16[2,32,64,256]{3,2,1,0:T(8,128)(2,1)} %get-tuple-element.364.refs_0_, bf16[2,32,64,256]{3,2,1,0:T(8,128)(2,1)} %get-tuple-element.365.refs_1_, f32[64,64]{1,0:T(8,128)S(1)} %get-tuple-element.366.refs_2_), custom_call_target="tpu_custom_call" | custom-call | flops 1073741824 | bytes 4194304 | tf_op jit(solution)/shard_map/cond/branch_0_fun/gram/pallas_call | solution.py:116
  207.8 3.9 %conditional.20 = (f32[8,64]{1,0:T(8,128)S(1)}) conditional(s32[]{:T(128)} %convert_element_type.4, (s32[5,2]{0,1:T(2,128)S(1)}, f32[4,2]{1,0:T(4,128)S(1)}, f32[8,64]{1,0:T(8,128)S(1)}, bf16[2,32,64,256]{3,2,1,0:T(8,128)(2,1)}, bf16[2,32,32,256]{3,2,1,0:T(8,128)(2,1)S(1)}, /*index=5*/bf16[2,32,32,256]{3,2,1,0:T(8,128)(2,1)}, ...), branch_computations={%region_18.19_spmd, %region_19.20_spmd} | conditional | flops 1073741824 | bytes 2097240 | solution.py:535
  215.2 3.9 %conditional.21 = (f32[8,64]{1,0:T(8,128)S(1)}) conditional(s32[]{:T(128)} %convert_element_type.4, (s32[5,2]{0,1:T(2,128)S(1)}, f32[4,2]{1,0:T(4,128)S(1)}, f32[8,64]{1,0:T(8,128)S(1)}, bf16[2,32,64,256]{3,2,1,0:T(8,128)(2,1)}, bf16[2,32,32,256]{3,2,1,0:T(8,128)(2,1)S(1)}, /*index=5*/bf16[2,32,32,256]{3,2,1,0:T(8,128)(2,1)}, ...), branch_computations={%region_20.21_spmd, %region_21.22_spmd} | conditional | flops 1073741824 | bytes 2097240 | solution.py:535
  (114 shorter events, 91.8 us)
Async XLA Ops:
  4.0 41.2 %collective-permute-start = (bf16[2,32,64,256]{3,2,1,0:T(8,128)(2,1)S(1)}, bf16[2,32,64,256]{3,2,1,0:T(8,128)(2,1)}, u32[]{:S(2)}, u32[]{:S(2)}) collective-permute-start(bf16[2,32,64,256]{3,2,1,0:T(8,128)(2,1)S(1)} %dress.2.refs_0_.refs_4_), channel_id=1, source_target_pairs={{0,1},{1,3},{2,0},{3,2},{4,5},{5,7},{6,4},{7,6},{8,9},{9,11},{10,8... | collective-permute-start | bytes 6291464 | tf_op jit(solution)/shard_map/ppermute | solution.py:389
  4.5 46.9 %collective-permute-start.4 = (bf16[2,32,64,256]{3,2,1,0:T(8,128)(2,1)S(1)}, bf16[2,32,64,256]{3,2,1,0:T(8,128)(2,1)}, u32[]{:S(2)}, u32[]{:S(2)}) collective-permute-start(bf16[2,32,64,256]{3,2,1,0:T(8,128)(2,1)S(1)} %dress.2.refs_0_.refs_4_), channel_id=1, source_target_pairs={{0,12},{3,7},{4,0},{7,11},{8,4},{11,15},{12,8},{15,3},{16,28},{19,... | collective-permute-start | bytes 6291464 | tf_op jit(solution)/shard_map/ppermute | solution.py:389
  45.2 6.2 %collective-permute-start.3 = (bf16[2,32,64,256]{3,2,1,0:T(8,128)(2,1)}, bf16[2,32,64,256]{3,2,1,0:T(8,128)(2,1)}, u32[]{:S(2)}, u32[]{:S(2)}) collective-permute-start(bf16[2,32,64,256]{3,2,1,0:T(8,128)(2,1)} %collective-permute-done), channel_id=1, source_target_pairs={{0,1},{3,2},{4,5},{7,6},{8,9},{11,10},{12,13},{15,14},{16,17},{19,... | collective-permute-start | bytes 6291464 | tf_op jit(solution)/shard_map/ppermute | solution.py:389
  47.8 26.4 %collective-permute-start.2 = (bf16[2,32,64,256]{3,2,1,0:T(8,128)(2,1)}, bf16[2,32,64,256]{3,2,1,0:T(8,128)(2,1)}, u32[]{:S(2)}, u32[]{:S(2)}) collective-permute-start(bf16[2,32,64,256]{3,2,1,0:T(8,128)(2,1)} %get-tuple-element.474.refs_1_.refs_5_), channel_id=1, source_target_pairs={{0,1},{1,3},{2,0},{3,2},{4,5},{5,7},{6,4},{7,6},{8,9},{9,11},{10,8... | collective-permute-start | bytes 6291464 | tf_op jit(solution)/shard_map/ppermute | solution.py:389
  47.8 32.5 %collective-permute-start.6 = (bf16[2,32,64,256]{3,2,1,0:T(8,128)(2,1)}, bf16[2,32,64,256]{3,2,1,0:T(8,128)(2,1)}, u32[]{:S(2)}, u32[]{:S(2)}) collective-permute-start(bf16[2,32,64,256]{3,2,1,0:T(8,128)(2,1)} %get-tuple-element.474.refs_1_.refs_5_), channel_id=1, source_target_pairs={{0,12},{3,7},{4,0},{7,11},{8,4},{11,15},{12,8},{15,3},{16,28},{19,... | collective-permute-start | bytes 6291464 | tf_op jit(solution)/shard_map/ppermute | solution.py:389
  74.2 6.2 %collective-permute-start.5 = (bf16[2,32,64,256]{3,2,1,0:T(8,128)(2,1)}, bf16[2,32,64,256]{3,2,1,0:T(8,128)(2,1)}, u32[]{:S(2)}, u32[]{:S(2)}) collective-permute-start(bf16[2,32,64,256]{3,2,1,0:T(8,128)(2,1)} %collective-permute-done.2), channel_id=1, source_target_pairs={{0,1},{3,2},{4,5},{7,6},{8,9},{11,10},{12,13},{15,14},{16,17},{19,... | collective-permute-start | bytes 6291464 | tf_op jit(solution)/shard_map/ppermute | solution.py:389
  76.8 26.4 %collective-permute-start.1 = (bf16[2,32,64,256]{3,2,1,0:T(8,128)(2,1)}, bf16[2,32,64,256]{3,2,1,0:T(8,128)(2,1)}, u32[]{:S(2)}, u32[]{:S(2)}) collective-permute-start(bf16[2,32,64,256]{3,2,1,0:T(8,128)(2,1)} %get-tuple-element.475.refs_2_.refs_6_), channel_id=1, source_target_pairs={{0,1},{1,3},{2,0},{3,2},{4,5},{5,7},{6,4},{7,6},{8,9},{9,11},{10,8... | collective-permute-start | bytes 6291464 | tf_op jit(solution)/shard_map/ppermute | solution.py:389
  76.8 35.3 %collective-permute-start.8 = (bf16[2,32,64,256]{3,2,1,0:T(8,128)(2,1)}, bf16[2,32,64,256]{3,2,1,0:T(8,128)(2,1)}, u32[]{:S(2)}, u32[]{:S(2)}) collective-permute-start(bf16[2,32,64,256]{3,2,1,0:T(8,128)(2,1)} %get-tuple-element.475.refs_2_.refs_6_), channel_id=1, source_target_pairs={{0,12},{3,7},{4,0},{7,11},{8,4},{11,15},{12,8},{15,3},{16,28},{19,... | collective-permute-start | bytes 6291464 | tf_op jit(solution)/shard_map/ppermute | solution.py:389
  103.1 9.0 %collective-permute-start.7 = (bf16[2,32,64,256]{3,2,1,0:T(8,128)(2,1)}, bf16[2,32,64,256]{3,2,1,0:T(8,128)(2,1)}, u32[]{:S(2)}, u32[]{:S(2)}) collective-permute-start(bf16[2,32,64,256]{3,2,1,0:T(8,128)(2,1)} %collective-permute-done.1), channel_id=1, source_target_pairs={{0,1},{3,2},{4,5},{7,6},{8,9},{11,10},{12,13},{15,14},{16,17},{19,... | collective-permute-start | bytes 6291464 | tf_op jit(solution)/shard_map/ppermute | solution.py:389
  105.7 11.9 %collective-permute-start.9 = (bf16[2,32,64,256]{3,2,1,0:T(8,128)(2,1)}, bf16[2,32,64,256]{3,2,1,0:T(8,128)(2,1)}, u32[]{:S(2)}, u32[]{:S(2)}) collective-permute-start(bf16[2,32,64,256]{3,2,1,0:T(8,128)(2,1)} %get-tuple-element.499.refs_3_.refs_7_), channel_id=1, source_target_pairs={{0,1},{3,2},{4,5},{7,6},{8,9},{11,10},{12,13},{15,14},{16,17},{19,... | collective-permute-start | bytes 6291464 | tf_op jit(solution)/shard_map/ppermute | solution.py:389
  108.5 26.4 %collective-permute-start.10 = (bf16[2,32,64,256]{3,2,1,0:T(8,128)(2,1)}, bf16[2,32,64,256]{3,2,1,0:T(8,128)(2,1)}, u32[]{:S(2)}, u32[]{:S(2)}) collective-permute-start(bf16[2,32,64,256]{3,2,1,0:T(8,128)(2,1)} %get-tuple-element.499.refs_3_.refs_7_), channel_id=1, source_target_pairs={{0,1},{1,3},{2,0},{3,2},{4,5},{5,7},{6,4},{7,6},{8,9},{9,11},{10,8... | collective-permute-start | bytes 6291464 | tf_op jit(solution)/shard_map/ppermute | solution.py:389
  108.5 35.6 %collective-permute-start.12 = (bf16[2,32,64,256]{3,2,1,0:T(8,128)(2,1)}, bf16[2,32,64,256]{3,2,1,0:T(8,128)(2,1)}, u32[]{:S(2)}, u32[]{:S(2)}) collective-permute-start(bf16[2,32,64,256]{3,2,1,0:T(8,128)(2,1)} %get-tuple-element.499.refs_3_.refs_7_), channel_id=1, source_target_pairs={{0,12},{3,7},{4,0},{7,11},{8,4},{11,15},{12,8},{15,3},{16,28},{19,... | collective-permute-start | bytes 6291464 | tf_op jit(solution)/shard_map/ppermute | solution.py:389
  134.8 11.9 %collective-permute-start.11 = (bf16[2,32,64,256]{3,2,1,0:T(8,128)(2,1)}, bf16[2,32,64,256]{3,2,1,0:T(8,128)(2,1)}, u32[]{:S(2)}, u32[]{:S(2)}) collective-permute-start(bf16[2,32,64,256]{3,2,1,0:T(8,128)(2,1)} %collective-permute-done.10), channel_id=1, source_target_pairs={{0,1},{3,2},{4,5},{7,6},{8,9},{11,10},{12,13},{15,14},{16,17},{19,... | collective-permute-start | bytes 6291464 | tf_op jit(solution)/shard_map/ppermute | solution.py:389
  137.4 17.4 %collective-permute-start.15 = (bf16[2,32,32,256]{3,2,1,0:T(8,128)(2,1)}, bf16[2,32,32,256]{3,2,1,0:T(8,128)(2,1)S(1)}, u32[]{:S(2)}, u32[]{:S(2)}) collective-permute-start(bf16[2,32,32,256]{3,2,1,0:T(8,128)(2,1)} %get-tuple-element.508), channel_id=1, source_target_pairs={{0,2},{3,1},{4,6},{7,5},{8,10},{11,9},{12,14},{15,13},{16,18},{19,... | collective-permute-start | bytes 3145736 | tf_op jit(solution)/shard_map/ppermute | solution.py:389
  138.8 35.0 %collective-permute-start.16 = (bf16[2,32,64,256]{3,2,1,0:T(8,128)(2,1)}, bf16[2,32,64,256]{3,2,1,0:T(8,128)(2,1)}, u32[]{:S(2)}, u32[]{:S(2)}) collective-permute-start(bf16[2,32,64,256]{3,2,1,0:T(8,128)(2,1)} %broadcast_select_fusion), channel_id=1, source_target_pairs={{0,2},{3,1},{4,6},{7,5},{8,10},{11,9},{12,14},{15,13},{16,18},{19,... | collective-permute-start | bytes 6291464 | tf_op jit(solution)/shard_map/ppermute | solution.py:389
  141.5 37.7 %collective-permute-start.18 = (bf16[2,32,64,256]{3,2,1,0:T(8,128)(2,1)}, bf16[2,32,64,256]{3,2,1,0:T(8,128)(2,1)}, u32[]{:S(2)}, u32[]{:S(2)}) collective-permute-start(bf16[2,32,64,256]{3,2,1,0:T(8,128)(2,1)} %collective-permute-done.4), channel_id=1, source_target_pairs={{0,1},{3,2},{4,5},{7,6},{8,9},{11,10},{12,13},{15,14},{16,17},{19,... | collective-permute-start | bytes 6291464 | tf_op jit(solution)/shard_map/ppermute | solution.py:389
  144.1 37.2 %collective-permute-start.17 = (bf16[2,32,64,256]{3,2,1,0:T(8,128)(2,1)}, bf16[2,32,64,256]{3,2,1,0:T(8,128)(2,1)}, u32[]{:S(2)}, u32[]{:S(2)}) collective-permute-start(bf16[2,32,64,256]{3,2,1,0:T(8,128)(2,1)} %collective-permute-done.8), channel_id=1, source_target_pairs={{0,1},{3,2},{4,5},{7,6},{8,9},{11,10},{12,13},{15,14},{16,17},{19,... | collective-permute-start | bytes 6291464 | tf_op jit(solution)/shard_map/ppermute | solution.py:389
  146.7 56.1 %collective-permute-start.19 = (bf16[2,32,64,256]{3,2,1,0:T(8,128)(2,1)}, bf16[2,32,64,256]{3,2,1,0:T(8,128)(2,1)}, u32[]{:S(2)}, u32[]{:S(2)}) collective-permute-start(bf16[2,32,64,256]{3,2,1,0:T(8,128)(2,1)} %collective-permute-done.6), channel_id=1, source_target_pairs={{0,1},{3,2},{4,5},{7,6},{8,9},{11,10},{12,13},{15,14},{16,17},{19,... | collective-permute-start | bytes 6291464 | tf_op jit(solution)/shard_map/ppermute | solution.py:389
  154.8 48.0 %collective-permute-start.14 = (bf16[2,32,64,256]{3,2,1,0:T(8,128)(2,1)}, bf16[2,32,64,256]{3,2,1,0:T(8,128)(2,1)}, u32[]{:S(2)}, u32[]{:S(2)}) collective-permute-start(bf16[2,32,64,256]{3,2,1,0:T(8,128)(2,1)} %collective-permute-done.12), channel_id=1, source_target_pairs={{0,1},{3,2},{4,5},{7,6},{8,9},{11,10},{12,13},{15,14},{16,17},{19,... | collective-permute-start | bytes 6291464 | tf_op jit(solution)/shard_map/ppermute | solution.py:389
  173.8 31.1 %collective-permute-start.13 = (bf16[2,32,32,256]{3,2,1,0:T(8,128)(2,1)}, bf16[2,32,32,256]{3,2,1,0:T(8,128)(2,1)}, u32[]{:S(2)}, u32[]{:S(2)}) collective-permute-start(bf16[2,32,32,256]{3,2,1,0:T(8,128)(2,1)} %get-tuple-element.505), channel_id=1, source_target_pairs={{0,2},{3,1},{4,6},{7,5},{8,10},{11,9},{12,14},{15,13},{16,18},{19,... | collective-permute-start | bytes 3145736 | tf_op jit(solution)/shard_map/ppermute | solution.py:389
  179.2 28.6 %collective-permute-start.20 = (bf16[1,2,4,128,256]{4,3,2,1,0:T(8,128)(2,1)}, bf16[1,2,4,128,256]{4,3,2,1,0:T(8,128)(2,1)}, u32[]{:S(2)}, u32[]{:S(2)}) collective-permute-start(bf16[1,2,4,128,256]{4,3,2,1,0:T(8,128)(2,1)} %get-tuple-element.517), channel_id=1, source_target_pairs={{0,2},{3,1},{4,6},{7,5},{8,10},{11,9},{12,14},{15,13},{16,18},{19,... | collective-permute-start | bytes 1572872 | tf_op jit(solution)/shard_map/ppermute | solution.py:389
  181.3 33.9 %collective-permute-start.22 = (bf16[1,2,4,128,256]{4,3,2,1,0:T(8,128)(2,1)}, bf16[1,2,4,128,256]{4,3,2,1,0:T(8,128)(2,1)}, u32[]{:S(2)}, u32[]{:S(2)}) collective-permute-start(bf16[1,2,4,128,256]{4,3,2,1,0:T(8,128)(2,1)} %get-tuple-element.519), channel_id=1, source_target_pairs={{0,2},{3,1},{4,6},{7,5},{8,10},{11,9},{12,14},{15,13},{16,18},{19,... | collective-permute-start | bytes 1572872 | tf_op jit(solution)/shard_map/ppermute | solution.py:389
  207.1 4.6 %collective-permute-start.21 = (f32[64,64]{1,0:T(8,128)S(1)}, f32[64,64]{1,0:T(8,128)S(1)}, u32[]{:S(2)}, u32[]{:S(2)}) collective-permute-start(f32[64,64]{1,0:T(8,128)S(1)} %get-tuple-element.604.refs_0_), channel_id=1, source_target_pairs={{2,13},{6,1},{10,5},{14,9},{18,29},{22,17},{26,21},{30,25}} | collective-permute-start | bytes 49160 | tf_op jit(solution)/shard_map/ppermute | solution.py:389
  227.5 4.5 %collective-permute-start.26 = (f32[8,64]{1,0:T(8,128)S(1)}, f32[8,64]{1,0:T(8,128)S(1)}, u32[]{:S(2)}, u32[]{:S(2)}) collective-permute-start(f32[8,64]{1,0:T(8,128)S(1)} %add.26), channel_id=1, source_target_pairs={{0,8},{1,9},{2,10},{3,11},{4,12},{5,13},{6,14},{7,15},{8,0},{9,1},... | collective-permute-start | bytes 6152 | tf_op jit(solution)/shard_map/ppermute | solution.py:372
  (9 other events, 60.5 us)

commit v2 on v1

--- a/solution.py
+++ b/solution.py
@@ -129,7 +129,7 @@
     )(*blocks, before)
 
 
-def box_kernel(counts, ins, scale, before, *refs):
+def box_kernel(counts, turned, ins, scale, *refs):
     groups = []
     for left_count, right_count, extra_count in counts:
         left, refs = refs[:left_count], refs[left_count:]
@@ -152,8 +152,12 @@
             start = 0
             for source in sources:
                 rows = source.shape[1]
+                target = start
+                if place % 2 == 1 and turned:
+                    target = lax.rem(start + ins[5, slot], held.shape[3])
+                    target = pl.multiple_of(target, rows)
                 pltpu.make_async_copy(
-                    source, held.at[slot, place, :, pl.ds(start, rows)], sems.at[slot]
+                    source, held.at[slot, place, :, pl.ds(target, rows)], sems.at[slot]
                 ).start()
                 start += rows
 
@@ -169,7 +173,7 @@
             nt_dot(jnp.concatenate([imag, -real], axis=1), other_side),
         )
 
-    out[...] = before[...]
+    out[...] = jnp.zeros_like(out)
     spot = lax.broadcasted_iota(jnp.int32, out.shape, 1)
     line = lax.broadcasted_iota(jnp.int32, out.shape, 0)
     for group in range(len(groups)):
@@ -192,7 +196,7 @@
             out[...] -= jnp.where(spot == ins[4, slot], added, 0.0)
 
 
-def box(groups, table, before):
+def box(groups, table, entries, turned=False):
     ins, scale = table
     slots = ins.shape[1]
     modes = groups[0][0][0].shape[3]
@@ -201,10 +205,12 @@
     smem = pl.BlockSpec(memory_space=pltpu.SMEM)
     vmem = pl.BlockSpec(memory_space=pltpu.VMEM)
     return pl.pallas_call(
-        functools.partial(box_kernel, [tuple(len(refs) for refs in group) for group in groups]),
-        in_specs=[smem, smem, vmem] + [pl.BlockSpec(memory_space=pl.ANY)] * len(arrays),
+        functools.partial(
+            box_kernel, [tuple(len(refs) for refs in group) for group in groups], turned
+        ),
+        in_specs=[smem, smem] + [pl.BlockSpec(memory_space=pl.ANY)] * len(arrays),
         out_specs=vmem,
-        out_shape=jax.ShapeDtypeStruct(before.shape, jnp.float32),
+        out_shape=jax.ShapeDtypeStruct((8, entries), jnp.float32),
         scratch_shapes=[
             pltpu.VMEM((slots, 4, 2, modes, modes), kind),
             pltpu.SemaphoreType.DMA((slots,)),
@@ -215,7 +221,7 @@
             transcendentals=0,
         ),
         name="box",
-    )(ins, scale, before, *arrays)
+    )(ins, scale, *arrays)
 
 
 def pick_kernel(count, upper, places, *refs):
@@ -284,7 +290,7 @@
     return jnp.concatenate([high, middle, low], axis=axis)
 
 
-def direct_kernel(swap, weight, ins, coef, entry, before, *refs):
+def direct_kernel(swap, weight, ins, coef, entry, *refs):
     tables, out, lines = refs[:-2], refs[-2], refs[-1]
     size = 2 * lines.shape[1]
     inserts = size // 2
@@ -302,7 +308,7 @@
         lines[pair * size + inserts : (pair + 1) * size] = lower[:, :inserts] - upper[:, inserts:]
     table = thirds(lines[...], 1)
     entries = out.shape[1]
-    total = before[...]
+    total = jnp.zeros(out.shape, jnp.float32)
     step = min(TERM_STEP, ins.shape[1])
     for start in range(0, ins.shape[1], step):
         span = slice(start, start + step)
@@ -340,15 +346,15 @@
     out[...] = total
 
 
-def direct(tables, pairs, swap, weight, ins, coef, entry, before):
+def direct(tables, pairs, swap, weight, ins, coef, entry, entries):
     size = tables[0].shape[0] // (2 if pairs == 3 else 1)
     smem = pl.BlockSpec(memory_space=pltpu.SMEM)
     vmem = pl.BlockSpec(memory_space=pltpu.VMEM)
     return pl.pallas_call(
         direct_kernel,
-        in_specs=[smem, smem] + [vmem] * (4 + len(tables)),
+        in_specs=[smem, smem] + [vmem] * (3 + len(tables)),
         out_specs=vmem,
-        out_shape=jax.ShapeDtypeStruct(before.shape, jnp.float32),
+        out_shape=jax.ShapeDtypeStruct((8, entries), jnp.float32),
         scratch_shapes=[pltpu.VMEM((pairs * size, size // 2), jnp.float32)],
         cost_estimate=pl.CostEstimate(
             flops=2 * pairs * size * size * ins.shape[1] * 3,
@@ -356,7 +362,7 @@
             transcendentals=0,
         ),
         name="direct",
-    )(swap, weight, ins, coef, entry, before, *tables)
+    )(swap, weight, ins, coef, entry, *tables)
 
 
 def after(value, *others):
@@ -469,21 +475,21 @@
     third_table = with_entry(role_table(third_swap), weight=third_weight, swap=third_swap)
     both_table = join(near_table, third_table)
     late_swap = by_role(0, 0, 1, 0)
-    late_tables = [
-        box_table(late_table[:, share], late_entry[share], late_coef[share], both_inner, late_swap)
-        for share in shares
-    ]
+    late_ins, late_scale = box_table(late_table, late_entry, late_coef, both_inner, late_swap)
+    turn = by_role(0, 0, fields.shape[2] // 2, 0) + jnp.zeros_like(late_entry)
+    late_ins = jnp.concatenate([late_ins, turn[None]])
+    late_tables = [(late_ins[:, share], late_scale[:, share]) for share in shares]
     main_scalars = (
         jnp.stack([jnp.int32(0), near_swap, third_swap, edge.astype(jnp.int32)]),
         jnp.concatenate([same_weight, near_weight, third_weight]),
     )
-    split_scalars = (jnp.zeros((4,), jnp.int32), split_weight)
+    split_scalars = (main_scalars[0], split_weight)
     direct_terms = (direct_ins.T, direct_coef[None], direct_entry[None])
     small = (
         near_table, third_table, both_table, late_tables, main_scalars, split_scalars, direct_terms
     )
 
-    total = box([(own, own, [])], same_table, jnp.zeros((8, entries), jnp.float32))
+    total = box([(own, own, [])], same_table, entries)
     table = jnp.zeros((2 * size, 3 * size), jnp.float32)
     (total, small, extra, split), _ = lax.optimization_barrier(((total, small, extra, split), near[0]))
     near_table, third_table, both_table, late_tables, main_scalars, split_scalars, direct_terms = small
@@ -506,40 +512,56 @@
         )
         early = (table,)
         if chunk == count - 2:
-            total = lax.cond(
+            total += lax.cond(
                 edge,
-                lambda o, m, k, t: t,
-                lambda o, m, k, t: box([(o, m, [])], k, t),
-                own, near[:-1] + [mate], near_table, after(total, table),
+                lambda o, m, k: jnp.zeros((8, entries), jnp.float32),
+                lambda o, m, k: box([(o, m, [])], k, entries),
+                own, near[:-1] + [mate], after(near_table, table),
             )
             early = (table, total)
     far_beside.append(move(after(far[-1], table), beside))
-    total = lax.cond(
+    third_table, both_table = after((third_table, both_table), table)
+    third = lax.cond(
         edge,
-        lambda o, a, z, c, k, j, t: box([(o, a, []), (a, z, [])], j, t),
-        lambda o, a, z, c, k, j, t: box([(o, c, [])], k, t),
-        own, near, far, near_beside, third_table, both_table, after(total, table),
+        lambda o, a, z, c, k, j: box([(o, a, []), (a, z, [])], j, entries),
+        lambda o, a, z, c, k, j: box([(o, c, [])], k, entries),
+        own, near, far, near_beside, third_table, both_table,
     )
-    total = direct([table], 3, *main_scalars, *direct_terms, total)
-    split_gram = after(jnp.zeros((size, size), jnp.float32), total)
+    main = direct([table], 3, *after(main_scalars, third), *direct_terms, entries)
+    branch = by_role(0, 1, 2, 0)
+    split_gram = after(jnp.zeros((size, size), jnp.float32), main)
     for piece, (j, start, _) in zip(split_in, cuts):
-        split_gram = lax.cond(
-            role == 1,
-            lambda v, lo, hi, t, start=start: gram([v, lo], 1, 1, t, start),
-            lambda v, lo, hi, t, start=start: gram([v, hi], 1, 1, t, start),
+        split_gram = lax.switch(
+            branch,
+            [
+                lambda v, lo, hi, t: jnp.zeros_like(t),
+                lambda v, lo, hi, t, start=start: gram([v, lo], 1, 1, t, start),
+                lambda v, lo, hi, t, start=start: gram([v, hi], 1, 1, t, start),
+            ],
             piece, far_beside[j], far_beside[half + j], split_gram,
         )
     split_other = move(split_gram, {2: lambda i: i - 5})
-    total = after(total, split_gram)
+    total += third + main
+    token = split_gram
+    late = []
     for number in range(len(shares)):
-        total = lax.cond(
-            role == 1,
-            lambda v, x, f, k, t: box([(v, f, [x])], k, t),
-            lambda v, x, f, k, t: box([(v, f[half:] + f[:half], [x])], k, t),
-            split_in, extra_in[number], far_beside, late_tables[number], total,
+        token = lax.cond(
+            edge,
+            lambda v, f, x, k: jnp.zeros((8, entries), jnp.float32),
+            lambda v, f, x, k: box([(v, f, [x])], k, entries, turned=True),
+            split_in, far_beside, extra_in[number], after(late_tables[number], token),
         )
+        late.append(token)
         if number == 0:
-            total = direct([split_gram, split_other], 1, *split_scalars, *direct_terms, total)
+            scalars = after(split_scalars, token)
+            token = lax.cond(
+                role == 1,
+                lambda a, b, k, d: direct([a, b], 1, *k, *d, entries),
+                lambda a, b, k, d: jnp.zeros((8, entries), jnp.float32),
+                split_gram, split_other, scalars, direct_terms,
+            )
+            late.append(token)
+    total += sum(late)
     summed = total_over(total, "tm") / devices
     mine = lax.dynamic_slice_in_dim(summed[:6], here * owned, owned, axis=1)
     return mine.reshape(3, 2, owned)

time: 234 us -> 222 us (0.949)
  Pallas kernels: 80.7 us -> 64.4 us
  starting transfers between devices: 56.5 us -> 63.8 us
    pallas_call x7 -> x4, Pallas kernels: 29.9 us -> 21.8 us  [gram(): pl.pallas_call(functools.partial(gram_kernel, count, left_count), grid=(r...]
    ppermute x4, starting transfers between devices: 0.76 us -> 8.26 us  [total_over(): lax.ppermute(value, axis, [(i, i ^ distance) for i in range(devices)])]
    pallas_call x4 -> x2, Pallas kernels: 25.5 us -> 19.7 us  [box(): pl.pallas_call(functools.partial(box_kernel, [tuple((len(refs) for refs i...]
    pallas_call x2 -> x1, Pallas kernels: 6.31 us -> 3.89 us  [direct(): pl.pallas_call(direct_kernel, in_specs=[smem, smem] + [vmem] * (3 + len(t...]
  transfers between devices with their start and end apart: 27 -> 27, of which waited for: 8 -> 9; matrix products, arithmetic and copies ran while one was open for 6% -> 5% of each run, Pallas kernels for 32% -> 27%
where the time goes in v2:
time: 222 us; the launch traced here: 221 us
  waiting for transfers between devices  79.4 us (36%)
  Pallas kernels  64.4 us (29%)
  starting transfers between devices  63.8 us (29%)
  other arithmetic  8 us (4%)
  local copies, waits for them, and re-layouts  4.37 us (2%)
    ppermute x23, waiting for transfers between devices, move(): return lax.ppermute(value, 'tm', route)  68.9 us
    ppermute x23, starting transfers between devices, move(): return lax.ppermute(value, 'tm', route)  55.5 us
    pallas_call x4, Pallas kernels, gram(): pl.pallas_call(functools.partial(gram_kernel, count, left_count), grid=(r...  21.8 us
    pallas_call x2, Pallas kernels, box(): pl.pallas_call(functools.partial(box_kernel, [tuple((len(refs) for refs i...  19.7 us
    pallas_call x2, Pallas kernels, dress(): pl.pallas_call(functools.partial(dress_kernel, [part * steps for part in...  16.4 us
    ppermute x4, waiting for transfers between devices, total_over(): lax.ppermute(value, axis, [(i, i ^ distance) for i in range(devices)])  10.5 us
    ppermute x4, starting transfers between devices, total_over(): lax.ppermute(value, axis, [(i, i ^ distance) for i in range(devices)])  8.26 us
    select_n x2, other arithmetic, local(): jnp.where(role == 0, own[half + j][:, :, start:start + length], own[j][:,...  5.45 us
  transfers between devices with their start and end apart: 27, of which 9 were waited for; matrix products, arithmetic and copies ran while one was open for 5% of the time, Pallas kernels for 27%

profile of v2, /device:TPU:0, one launch (start us, length us, event | category | flops | bytes accessed | tf_op | source)
XLA Modules:
  0.0 220.7 jit_solution(13320996678610424752)
XLA Ops:
  0.0 4.0 %dress.2.refs_0_.refs_4_ = bf16[2,32,64,256]{3,2,1,0:T(8,128)(2,1)S(1)} custom-call(bf16[2,32,256,256]{3,2,1,0:T(8,128)(2,1)} %bitcast.44, bf16[2,256,256]{2,1,0:T(8,128)(2,1)} %bitcast.46), custom_call_target="tpu_custom_call" | custom-call | flops 2147483648 | bytes 4194304 | tf_op jit(solution)/shard_map/dress/pallas_call | solution.py:66
  4.5 6.5 %collective-permute-start.4 = (bf16[2,32,64,256]{3,2,1,0:T(8,128)(2,1)S(1)}, bf16[2,32,64,256]{3,2,1,0:T(8,128)(2,1)}, u32[]{:S(2)}, u32[]{:S(2)}) collective-permute-start(bf16[2,32,64,256]{3,2,1,0:T(8,128)(2,1)S(1)} %dress.2.refs_0_.refs_4_), channel_id=1, source_target_pairs={{0,12},{3,7},{4,0},{7,11},{8,4},{11,15},{12,8},{15,3},{16,28},{19,... | collective-permute-start | bytes 6291464 | tf_op jit(solution)/shard_map/ppermute | solution.py:395
  12.6 12.4 %dress.3 = (bf16[2,32,64,256]{3,2,1,0:T(8,128)(2,1)}, bf16[2,32,64,256]{3,2,1,0:T(8,128)(2,1)}, bf16[2,32,64,256]{3,2,1,0:T(8,128)(2,1)}) custom-call(bf16[2,32,256,256]{3,2,1,0:T(8,128)(2,1)} %bitcast.45, bf16[2,256,256]{2,1,0:T(8,128)(2,1)} %bitcast.47), custom_call_target="tpu_custom_call" | custom-call | flops 6442450944 | bytes 12582912 | tf_op jit(solution)/shard_map/dress/pallas_call | solution.py:66
  30.4 3.9 %slice_select_fusion = (bf16[2,32,32,256]{3,2,1,0:T(8,128)(2,1)}, bf16[2,32,32,256]{3,2,1,0:T(8,128)(2,1)}) fusion(bf16[2,32,64,256]{3,2,1,0:T(8,128)(2,1)} %get-tuple-element.430.refs_1_.refs_5_, bf16[2,32,64,256]{3,2,1,0:T(8,128)(2,1)} %get-tuple-element.443.refs_3_.refs_7_, pred[]{:T(512)S(6)} %eq.18), kind=kLoop, calls=%fused_computation.2 | loop fusion | flops 1048576 | bytes 6291457 | tf_op jit(solution)/shard_map/jit(_where)/select_n | solution.py:432
  35.8 7.9 %box.11 = f32[8,64]{1,0:T(8,128)} custom-call(s32[5,8]{1,0:T(8,128)} %get-tuple-element.512.ins, f32[4,8]{1,0:T(4,128)} %get-tuple-element.505.scale, bf16[2,32,64,256]{3,2,1,0:T(8,128)(2,1)S(1)} %dress.2.refs_0_.refs_4_, bf16[2,32,64,256]{3,2,1,0:T(8,128)(2,1)} %get-tuple-element.430.refs_1_.refs_5_, ...), custom_call_target="tpu_custom_call" | custom-call | flops 4294967296 | bytes 8388608 | tf_op jit(solution)/shard_map/box/pallas_call | solution.py:207
  50.0 5.9 %conditional.12 = (f32[128,192]{1,0:T(8,128)S(1)}) conditional(s32[]{:T(128)} %convert_element_type.4, (bf16[2,32,64,256]{3,2,1,0:T(8,128)(2,1)S(1)}, bf16[2,32,64,256]{3,2,1,0:T(8,128)(2,1)}, bf16[2,32,64,256]{3,2,1,0:T(8,128)(2,1)}) %tuple.112, (bf16[2,32,64,256]{3,2,1,0:T(8,128)(2,1)S(1)}, bf16[2,32,64,256]{3,2,1,0:T(8,128)(2,1)}, ...), branch_computations={%region_0.1_spmd, %region_1.2_spmd} | conditional | flops 6442450944 | bytes 6389772 | solution.py:507
  50.7 5.3 %gram.15 = f32[128,192]{1,0:T(8,128)S(1)} custom-call(bf16[2,32,64,256]{3,2,1,0:T(8,128)(2,1)S(1)} %get-tuple-element.251.refs_0_, bf16[2,32,64,256]{3,2,1,0:T(8,128)(2,1)} %get-tuple-element.252.refs_1_, bf16[2,32,64,256]{3,2,1,0:T(8,128)(2,1)} %get-tuple-element.253.refs_2_, f32[128,192]{1,0:T(8,128)} %broadcast_in_dim.9.refs_3_), custom_call_target="tpu_custom_call" | custom-call | flops 6442450944 | bytes 6291456 | tf_op jit(solution)/shard_map/cond/branch_1_fun/gram/pallas_call | solution.py:116
  56.0 16.8 %collective-permute-done.2 = bf16[2,32,64,256]{3,2,1,0:T(8,128)(2,1)} collective-permute-done((bf16[2,32,64,256]{3,2,1,0:T(8,128)(2,1)}, bf16[2,32,64,256]{3,2,1,0:T(8,128)(2,1)}, u32[]{:S(2)}, u32[]{:S(2)}) %collective-permute-start.2) | collective-permute-done | bytes 2097184 | tf_op jit(solution)/shard_map/ppermute | solution.py:395
  79.0 5.5 %conditional.13 = (f32[128,192]{1,0:T(8,128)S(1)}) conditional(s32[]{:T(128)} %convert_element_type.4, (bf16[2,32,64,256]{3,2,1,0:T(8,128)(2,1)}, bf16[2,32,64,256]{3,2,1,0:T(8,128)(2,1)}, bf16[2,32,64,256]{3,2,1,0:T(8,128)(2,1)}, f32[128,192]{1,0:T(8,128)S(1)}) %tuple.115, (bf16[2,32,64,256]{3,2,1,0:T(8,128)(2,1)}, ...), branch_computations={%region_2.3_spmd, %region_3.4_spmd} | conditional | flops 6442450944 | bytes 6291464 | solution.py:507
  79.0 5.5 %gram.17 = f32[128,192]{1,0:T(8,128)S(1)} custom-call(bf16[2,32,64,256]{3,2,1,0:T(8,128)(2,1)} %get-tuple-element.258.refs_0_, bf16[2,32,64,256]{3,2,1,0:T(8,128)(2,1)} %get-tuple-element.270.refs_1_, bf16[2,32,64,256]{3,2,1,0:T(8,128)(2,1)} %get-tuple-element.272.refs_2_, f32[128,192]{1,0:T(8,128)S(1)} %get-tuple-element.274.refs_3_), custom_call_target="tpu_custom_call" | custom-call | flops 6442450944 | bytes 6291456 | tf_op jit(solution)/shard_map/cond/branch_1_fun/gram/pallas_call | solution.py:116
  84.5 17.2 %collective-permute-done.1 = bf16[2,32,64,256]{3,2,1,0:T(8,128)(2,1)} collective-permute-done((bf16[2,32,64,256]{3,2,1,0:T(8,128)(2,1)}, bf16[2,32,64,256]{3,2,1,0:T(8,128)(2,1)}, u32[]{:S(2)}, u32[]{:S(2)}) %collective-permute-start.1) | collective-permute-done | bytes 2097184 | tf_op jit(solution)/shard_map/ppermute | solution.py:395
  110.5 5.5 %conditional.14 = (f32[128,192]{1,0:T(8,128)S(1)}) conditional(s32[]{:T(128)} %convert_element_type.4, (bf16[2,32,64,256]{3,2,1,0:T(8,128)(2,1)}, bf16[2,32,64,256]{3,2,1,0:T(8,128)(2,1)}, bf16[2,32,64,256]{3,2,1,0:T(8,128)(2,1)}, f32[128,192]{1,0:T(8,128)S(1)}) %tuple.118, (bf16[2,32,64,256]{3,2,1,0:T(8,128)(2,1)}, ...), branch_computations={%region_4.5_spmd, %region_5.6_spmd} | conditional | flops 6442450944 | bytes 6291464 | solution.py:507
  110.6 5.5 %gram.19 = f32[128,192]{1,0:T(8,128)S(1)} custom-call(bf16[2,32,64,256]{3,2,1,0:T(8,128)(2,1)} %get-tuple-element.280.refs_0_, bf16[2,32,64,256]{3,2,1,0:T(8,128)(2,1)} %get-tuple-element.281.refs_1_, bf16[2,32,64,256]{3,2,1,0:T(8,128)(2,1)} %get-tuple-element.282.refs_2_, f32[128,192]{1,0:T(8,128)S(1)} %get-tuple-element.283.refs_3_), custom_call_target="tpu_custom_call" | custom-call | flops 6442450944 | bytes 6291456 | tf_op jit(solution)/shard_map/cond/branch_1_fun/gram/pallas_call | solution.py:116
  116.8 16.5 %collective-permute-done.10 = bf16[2,32,64,256]{3,2,1,0:T(8,128)(2,1)} collective-permute-done((bf16[2,32,64,256]{3,2,1,0:T(8,128)(2,1)}, bf16[2,32,64,256]{3,2,1,0:T(8,128)(2,1)}, u32[]{:S(2)}, u32[]{:S(2)}) %collective-permute-start.10) | collective-permute-done | bytes 2097184 | tf_op jit(solution)/shard_map/ppermute | solution.py:395
  147.7 5.5 %conditional.16 = (f32[128,192]{1,0:T(8,128)S(1)}) conditional(s32[]{:T(128)} %convert_element_type.4, (bf16[2,32,64,256]{3,2,1,0:T(8,128)(2,1)}, bf16[2,32,64,256]{3,2,1,0:T(8,128)(2,1)}, bf16[2,32,64,256]{3,2,1,0:T(8,128)(2,1)}, f32[128,192]{1,0:T(8,128)S(1)}) %tuple.125, (bf16[2,32,64,256]{3,2,1,0:T(8,128)(2,1)}, ...), branch_computations={%region_8.9_spmd, %region_9.10_spmd} | conditional | flops 6442450944 | bytes 6291464 | solution.py:507
  147.7 5.5 %gram.21 = f32[128,192]{1,0:T(8,128)S(1)} custom-call(bf16[2,32,64,256]{3,2,1,0:T(8,128)(2,1)} %get-tuple-element.298.refs_0_, bf16[2,32,64,256]{3,2,1,0:T(8,128)(2,1)} %get-tuple-element.299.refs_1_, bf16[2,32,64,256]{3,2,1,0:T(8,128)(2,1)} %get-tuple-element.300.refs_2_, f32[128,192]{1,0:T(8,128)S(1)} %get-tuple-element.301.refs_3_), custom_call_target="tpu_custom_call" | custom-call | flops 6442450944 | bytes 6291456 | tf_op jit(solution)/shard_map/cond/branch_1_fun/gram/pallas_call | solution.py:116
  155.9 16.4 %collective-permute-done.16 = bf16[2,32,64,256]{3,2,1,0:T(8,128)(2,1)} collective-permute-done((bf16[2,32,64,256]{3,2,1,0:T(8,128)(2,1)}, bf16[2,32,64,256]{3,2,1,0:T(8,128)(2,1)}, u32[]{:S(2)}, u32[]{:S(2)}) %collective-permute-start.16) | collective-permute-done | bytes 2097184 | tf_op jit(solution)/shard_map/ppermute | solution.py:395
  172.3 5.3 %collective-permute-start.13 = (bf16[2,32,32,256]{3,2,1,0:T(8,128)(2,1)}, bf16[2,32,32,256]{3,2,1,0:T(8,128)(2,1)}, u32[]{:S(2)}, u32[]{:S(2)}) collective-permute-start(bf16[2,32,32,256]{3,2,1,0:T(8,128)(2,1)} %get-tuple-element.463), channel_id=1, source_target_pairs={{0,2},{3,1},{4,6},{7,5},{8,10},{11,9},{12,14},{15,13},{16,18},{19,... | collective-permute-start | bytes 3145736 | tf_op jit(solution)/shard_map/ppermute | solution.py:395
  181.9 12.0 %conditional.17 = (f32[8,64]{1,0:T(8,128)S(1)}) conditional(s32[]{:T(128)} %convert_element_type.4, (s32[5,8]{1,0:T(8,128)S(1)}, f32[4,8]{1,0:T(4,128)S(1)}, bf16[2,32,64,256]{3,2,1,0:T(8,128)(2,1)S(1)}, bf16[2,32,64,256]{3,2,1,0:T(8,128)(2,1)}, bf16[2,32,64,256]{3,2,1,0:T(8,128)(2,1)}, /*index=5*/bf16[2,32,64,256]{3,2,1,0:T(8,128)(2,1)}, ...), branch_computations={%region_10.11_spmd, %region_11.12_spmd} | conditional | flops 8589934592 | bytes 16777224 | solution.py:524
  181.9 11.8 %box.8 = f32[8,64]{1,0:T(8,128)S(1)} custom-call(s32[5,16]{1,0:T(8,128)S(1)} %get-tuple-element.312.ins, f32[4,16]{1,0:T(4,128)S(1)} %get-tuple-element.313.scale, bf16[2,32,64,256]{3,2,1,0:T(8,128)(2,1)S(1)} %get-tuple-element.314.refs_0_, bf16[2,32,64,256]{3,2,1,0:T(8,128)(2,1)} %get-tuple-element.315.refs_1_, ...), custom_call_target="tpu_custom_call" | custom-call | flops 8589934592 | bytes 16777216 | tf_op jit(solution)/shard_map/cond/branch_1_fun/box/pallas_call | solution.py:207
  193.9 3.9 %direct.3 = f32[8,64]{1,0:T(8,128)} custom-call(s32[4]{0:T(128)S(1)} %pad_add_fusion.3.swap, f32[9]{0:T(128)} %concatenate.30.weight, s32[4,4096]{1,0:T(4,128)S(1)} %bitcast.55, f32[1,4096]{1,0:T(1,128)S(1)} %bitcast.57, s32[1,4096]{1,0:T(1,128)S(1)} %bitcast.59, f32[128,192]{1,0:T(8,128)S(1)} %get-tuple-element.517.refs_0_), custom_call_target="tpu_custom_call" | custom-call | flops 301989888 | bytes 163840 | tf_op jit(solution)/shard_map/direct/pallas_call | solution.py:353
  201.2 6.3 %collective-permute-start.23 = (f32[8,64]{1,0:T(8,128)S(1)}, f32[8,64]{1,0:T(8,128)S(1)}, u32[]{:S(2)}, u32[]{:S(2)}) collective-permute-start(f32[8,64]{1,0:T(8,128)S(1)} %add_add_fusion.2), channel_id=1, source_target_pairs={{0,1},{1,0},{2,3},{3,2},{4,5},{5,4},{6,7},{7,6},{8,9},{9,8},{10,11... | collective-permute-start | bytes 6152 | tf_op jit(solution)/shard_map/ppermute | solution.py:378
  208.3 3.6 %collective-permute-done.24 = f32[8,64]{1,0:T(8,128)S(1)} collective-permute-done((f32[8,64]{1,0:T(8,128)S(1)}, f32[8,64]{1,0:T(8,128)S(1)}, u32[]{:S(2)}, u32[]{:S(2)}) %collective-permute-start.24) | collective-permute-done | bytes 2080 | tf_op jit(solution)/shard_map/ppermute | solution.py:378
  211.9 3.6 %collective-permute-done.25 = f32[8,64]{1,0:T(8,128)S(1)} collective-permute-done((f32[8,64]{1,0:T(8,128)S(1)}, f32[8,64]{1,0:T(8,128)S(1)}, u32[]{:S(2)}, u32[]{:S(2)}) %collective-permute-start.25) | collective-permute-done | bytes 2080 | tf_op jit(solution)/shard_map/ppermute | solution.py:378
  (118 shorter events, 62.2 us)
Async XLA Ops:
  4.0 39.7 %collective-permute-start = (bf16[2,32,64,256]{3,2,1,0:T(8,128)(2,1)S(1)}, bf16[2,32,64,256]{3,2,1,0:T(8,128)(2,1)}, u32[]{:S(2)}, u32[]{:S(2)}) collective-permute-start(bf16[2,32,64,256]{3,2,1,0:T(8,128)(2,1)S(1)} %dress.2.refs_0_.refs_4_), channel_id=1, source_target_pairs={{0,1},{1,3},{2,0},{3,2},{4,5},{5,7},{6,4},{7,6},{8,9},{9,11},{10,8... | collective-permute-start | bytes 6291464 | tf_op jit(solution)/shard_map/ppermute | solution.py:395
  4.5 45.5 %collective-permute-start.4 = (bf16[2,32,64,256]{3,2,1,0:T(8,128)(2,1)S(1)}, bf16[2,32,64,256]{3,2,1,0:T(8,128)(2,1)}, u32[]{:S(2)}, u32[]{:S(2)}) collective-permute-start(bf16[2,32,64,256]{3,2,1,0:T(8,128)(2,1)S(1)} %dress.2.refs_0_.refs_4_), channel_id=1, source_target_pairs={{0,12},{3,7},{4,0},{7,11},{8,4},{11,15},{12,8},{15,3},{16,28},{19,... | collective-permute-start | bytes 6291464 | tf_op jit(solution)/shard_map/ppermute | solution.py:395
  43.7 6.3 %collective-permute-start.3 = (bf16[2,32,64,256]{3,2,1,0:T(8,128)(2,1)}, bf16[2,32,64,256]{3,2,1,0:T(8,128)(2,1)}, u32[]{:S(2)}, u32[]{:S(2)}) collective-permute-start(bf16[2,32,64,256]{3,2,1,0:T(8,128)(2,1)} %collective-permute-done), channel_id=1, source_target_pairs={{0,1},{3,2},{4,5},{7,6},{8,9},{11,10},{12,13},{15,14},{16,17},{19,... | collective-permute-start | bytes 6291464 | tf_op jit(solution)/shard_map/ppermute | solution.py:395
  46.4 26.4 %collective-permute-start.2 = (bf16[2,32,64,256]{3,2,1,0:T(8,128)(2,1)}, bf16[2,32,64,256]{3,2,1,0:T(8,128)(2,1)}, u32[]{:S(2)}, u32[]{:S(2)}) collective-permute-start(bf16[2,32,64,256]{3,2,1,0:T(8,128)(2,1)} %get-tuple-element.430.refs_1_.refs_5_), channel_id=1, source_target_pairs={{0,1},{1,3},{2,0},{3,2},{4,5},{5,7},{6,4},{7,6},{8,9},{9,11},{10,8... | collective-permute-start | bytes 6291464 | tf_op jit(solution)/shard_map/ppermute | solution.py:395
  46.4 32.5 %collective-permute-start.6 = (bf16[2,32,64,256]{3,2,1,0:T(8,128)(2,1)}, bf16[2,32,64,256]{3,2,1,0:T(8,128)(2,1)}, u32[]{:S(2)}, u32[]{:S(2)}) collective-permute-start(bf16[2,32,64,256]{3,2,1,0:T(8,128)(2,1)} %get-tuple-element.430.refs_1_.refs_5_), channel_id=1, source_target_pairs={{0,12},{3,7},{4,0},{7,11},{8,4},{11,15},{12,8},{15,3},{16,28},{19,... | collective-permute-start | bytes 6291464 | tf_op jit(solution)/shard_map/ppermute | solution.py:395
  72.8 6.2 %collective-permute-start.5 = (bf16[2,32,64,256]{3,2,1,0:T(8,128)(2,1)}, bf16[2,32,64,256]{3,2,1,0:T(8,128)(2,1)}, u32[]{:S(2)}, u32[]{:S(2)}) collective-permute-start(bf16[2,32,64,256]{3,2,1,0:T(8,128)(2,1)} %collective-permute-done.2), channel_id=1, source_target_pairs={{0,1},{3,2},{4,5},{7,6},{8,9},{11,10},{12,13},{15,14},{16,17},{19,... | collective-permute-start | bytes 6291464 | tf_op jit(solution)/shard_map/ppermute | solution.py:395
  75.4 26.4 %collective-permute-start.1 = (bf16[2,32,64,256]{3,2,1,0:T(8,128)(2,1)}, bf16[2,32,64,256]{3,2,1,0:T(8,128)(2,1)}, u32[]{:S(2)}, u32[]{:S(2)}) collective-permute-start(bf16[2,32,64,256]{3,2,1,0:T(8,128)(2,1)} %get-tuple-element.431.refs_2_.refs_6_), channel_id=1, source_target_pairs={{0,1},{1,3},{2,0},{3,2},{4,5},{5,7},{6,4},{7,6},{8,9},{9,11},{10,8... | collective-permute-start | bytes 6291464 | tf_op jit(solution)/shard_map/ppermute | solution.py:395
  75.4 35.2 %collective-permute-start.8 = (bf16[2,32,64,256]{3,2,1,0:T(8,128)(2,1)}, bf16[2,32,64,256]{3,2,1,0:T(8,128)(2,1)}, u32[]{:S(2)}, u32[]{:S(2)}) collective-permute-start(bf16[2,32,64,256]{3,2,1,0:T(8,128)(2,1)} %get-tuple-element.431.refs_2_.refs_6_), channel_id=1, source_target_pairs={{0,12},{3,7},{4,0},{7,11},{8,4},{11,15},{12,8},{15,3},{16,28},{19,... | collective-permute-start | bytes 6291464 | tf_op jit(solution)/shard_map/ppermute | solution.py:395
  101.7 8.8 %collective-permute-start.7 = (bf16[2,32,64,256]{3,2,1,0:T(8,128)(2,1)}, bf16[2,32,64,256]{3,2,1,0:T(8,128)(2,1)}, u32[]{:S(2)}, u32[]{:S(2)}) collective-permute-start(bf16[2,32,64,256]{3,2,1,0:T(8,128)(2,1)} %collective-permute-done.1), channel_id=1, source_target_pairs={{0,1},{3,2},{4,5},{7,6},{8,9},{11,10},{12,13},{15,14},{16,17},{19,... | collective-permute-start | bytes 6291464 | tf_op jit(solution)/shard_map/ppermute | solution.py:395
  104.3 11.7 %collective-permute-start.9 = (bf16[2,32,64,256]{3,2,1,0:T(8,128)(2,1)}, bf16[2,32,64,256]{3,2,1,0:T(8,128)(2,1)}, u32[]{:S(2)}, u32[]{:S(2)}) collective-permute-start(bf16[2,32,64,256]{3,2,1,0:T(8,128)(2,1)} %get-tuple-element.443.refs_3_.refs_7_), channel_id=1, source_target_pairs={{0,1},{3,2},{4,5},{7,6},{8,9},{11,10},{12,13},{15,14},{16,17},{19,... | collective-permute-start | bytes 6291464 | tf_op jit(solution)/shard_map/ppermute | solution.py:395
  106.9 26.4 %collective-permute-start.10 = (bf16[2,32,64,256]{3,2,1,0:T(8,128)(2,1)}, bf16[2,32,64,256]{3,2,1,0:T(8,128)(2,1)}, u32[]{:S(2)}, u32[]{:S(2)}) collective-permute-start(bf16[2,32,64,256]{3,2,1,0:T(8,128)(2,1)} %get-tuple-element.443.refs_3_.refs_7_), channel_id=1, source_target_pairs={{0,1},{1,3},{2,0},{3,2},{4,5},{5,7},{6,4},{7,6},{8,9},{9,11},{10,8... | collective-permute-start | bytes 6291464 | tf_op jit(solution)/shard_map/ppermute | solution.py:395
  106.9 35.5 %collective-permute-start.12 = (bf16[2,32,64,256]{3,2,1,0:T(8,128)(2,1)}, bf16[2,32,64,256]{3,2,1,0:T(8,128)(2,1)}, u32[]{:S(2)}, u32[]{:S(2)}) collective-permute-start(bf16[2,32,64,256]{3,2,1,0:T(8,128)(2,1)} %get-tuple-element.443.refs_3_.refs_7_), channel_id=1, source_target_pairs={{0,12},{3,7},{4,0},{7,11},{8,4},{11,15},{12,8},{15,3},{16,28},{19,... | collective-permute-start | bytes 6291464 | tf_op jit(solution)/shard_map/ppermute | solution.py:395
  133.3 11.8 %collective-permute-start.11 = (bf16[2,32,64,256]{3,2,1,0:T(8,128)(2,1)}, bf16[2,32,64,256]{3,2,1,0:T(8,128)(2,1)}, u32[]{:S(2)}, u32[]{:S(2)}) collective-permute-start(bf16[2,32,64,256]{3,2,1,0:T(8,128)(2,1)} %collective-permute-done.10), channel_id=1, source_target_pairs={{0,1},{3,2},{4,5},{7,6},{8,9},{11,10},{12,13},{15,14},{16,17},{19,... | collective-permute-start | bytes 6291464 | tf_op jit(solution)/shard_map/ppermute | solution.py:395
  135.9 17.3 %collective-permute-start.15 = (bf16[2,32,32,256]{3,2,1,0:T(8,128)(2,1)}, bf16[2,32,32,256]{3,2,1,0:T(8,128)(2,1)S(1)}, u32[]{:S(2)}, u32[]{:S(2)}) collective-permute-start(bf16[2,32,32,256]{3,2,1,0:T(8,128)(2,1)} %get-tuple-element.466), channel_id=1, source_target_pairs={{0,2},{3,1},{4,6},{7,5},{8,10},{11,9},{12,14},{15,13},{16,18},{19,... | collective-permute-start | bytes 3145736 | tf_op jit(solution)/shard_map/ppermute | solution.py:395
  137.3 35.0 %collective-permute-start.16 = (bf16[2,32,64,256]{3,2,1,0:T(8,128)(2,1)}, bf16[2,32,64,256]{3,2,1,0:T(8,128)(2,1)}, u32[]{:S(2)}, u32[]{:S(2)}) collective-permute-start(bf16[2,32,64,256]{3,2,1,0:T(8,128)(2,1)} %broadcast_select_fusion), channel_id=1, source_target_pairs={{0,2},{3,1},{4,6},{7,5},{8,10},{11,9},{12,14},{15,13},{16,18},{19,... | collective-permute-start | bytes 6291464 | tf_op jit(solution)/shard_map/ppermute | solution.py:395
  139.9 37.8 %collective-permute-start.17 = (bf16[2,32,64,256]{3,2,1,0:T(8,128)(2,1)}, bf16[2,32,64,256]{3,2,1,0:T(8,128)(2,1)}, u32[]{:S(2)}, u32[]{:S(2)}) collective-permute-start(bf16[2,32,64,256]{3,2,1,0:T(8,128)(2,1)} %collective-permute-done.4), channel_id=1, source_target_pairs={{0,1},{3,2},{4,5},{7,6},{8,9},{11,10},{12,13},{15,14},{16,17},{19,... | collective-permute-start | bytes 6291464 | tf_op jit(solution)/shard_map/ppermute | solution.py:395
  142.5 37.2 %collective-permute-start.18 = (bf16[2,32,64,256]{3,2,1,0:T(8,128)(2,1)}, bf16[2,32,64,256]{3,2,1,0:T(8,128)(2,1)}, u32[]{:S(2)}, u32[]{:S(2)}) collective-permute-start(bf16[2,32,64,256]{3,2,1,0:T(8,128)(2,1)} %collective-permute-done.8), channel_id=1, source_target_pairs={{0,1},{3,2},{4,5},{7,6},{8,9},{11,10},{12,13},{15,14},{16,17},{19,... | collective-permute-start | bytes 6291464 | tf_op jit(solution)/shard_map/ppermute | solution.py:395
  145.1 52.7 %collective-permute-start.14 = (bf16[2,32,64,256]{3,2,1,0:T(8,128)(2,1)}, bf16[2,32,64,256]{3,2,1,0:T(8,128)(2,1)}, u32[]{:S(2)}, u32[]{:S(2)}) collective-permute-start(bf16[2,32,64,256]{3,2,1,0:T(8,128)(2,1)} %collective-permute-done.6), channel_id=1, source_target_pairs={{0,1},{3,2},{4,5},{7,6},{8,9},{11,10},{12,13},{15,14},{16,17},{19,... | collective-permute-start | bytes 6291464 | tf_op jit(solution)/shard_map/ppermute | solution.py:395
  153.3 44.6 %collective-permute-start.19 = (bf16[2,32,64,256]{3,2,1,0:T(8,128)(2,1)}, bf16[2,32,64,256]{3,2,1,0:T(8,128)(2,1)}, u32[]{:S(2)}, u32[]{:S(2)}) collective-permute-start(bf16[2,32,64,256]{3,2,1,0:T(8,128)(2,1)} %collective-permute-done.12), channel_id=1, source_target_pairs={{0,1},{3,2},{4,5},{7,6},{8,9},{11,10},{12,13},{15,14},{16,17},{19,... | collective-permute-start | bytes 6291464 | tf_op jit(solution)/shard_map/ppermute | solution.py:395
  172.3 25.6 %collective-permute-start.13 = (bf16[2,32,32,256]{3,2,1,0:T(8,128)(2,1)}, bf16[2,32,32,256]{3,2,1,0:T(8,128)(2,1)}, u32[]{:S(2)}, u32[]{:S(2)}) collective-permute-start(bf16[2,32,32,256]{3,2,1,0:T(8,128)(2,1)} %get-tuple-element.463), channel_id=1, source_target_pairs={{0,2},{3,1},{4,6},{7,5},{8,10},{11,9},{12,14},{15,13},{16,18},{19,... | collective-permute-start | bytes 3145736 | tf_op jit(solution)/shard_map/ppermute | solution.py:395
  177.6 21.0 %collective-permute-start.20 = (bf16[1,2,4,128,256]{4,3,2,1,0:T(8,128)(2,1)}, bf16[1,2,4,128,256]{4,3,2,1,0:T(8,128)(2,1)}, u32[]{:S(2)}, u32[]{:S(2)}) collective-permute-start(bf16[1,2,4,128,256]{4,3,2,1,0:T(8,128)(2,1)} %get-tuple-element.476), channel_id=1, source_target_pairs={{0,2},{3,1},{4,6},{7,5},{8,10},{11,9},{12,14},{15,13},{16,18},{19,... | collective-permute-start | bytes 1572872 | tf_op jit(solution)/shard_map/ppermute | solution.py:395
  179.7 20.8 %collective-permute-start.22 = (bf16[1,2,4,128,256]{4,3,2,1,0:T(8,128)(2,1)}, bf16[1,2,4,128,256]{4,3,2,1,0:T(8,128)(2,1)}, u32[]{:S(2)}, u32[]{:S(2)}) collective-permute-start(bf16[1,2,4,128,256]{4,3,2,1,0:T(8,128)(2,1)} %get-tuple-element.486), channel_id=1, source_target_pairs={{0,2},{3,1},{4,6},{7,5},{8,10},{11,9},{12,14},{15,13},{16,18},{19,... | collective-permute-start | bytes 1572872 | tf_op jit(solution)/shard_map/ppermute | solution.py:395
  201.2 7.1 %collective-permute-start.23 = (f32[8,64]{1,0:T(8,128)S(1)}, f32[8,64]{1,0:T(8,128)S(1)}, u32[]{:S(2)}, u32[]{:S(2)}) collective-permute-start(f32[8,64]{1,0:T(8,128)S(1)} %add_add_fusion.2), channel_id=1, source_target_pairs={{0,1},{1,0},{2,3},{3,2},{4,5},{5,4},{6,7},{7,6},{8,9},{9,8},{10,11... | collective-permute-start | bytes 6152 | tf_op jit(solution)/shard_map/ppermute | solution.py:378
  215.5 4.5 %collective-permute-start.26 = (f32[8,64]{1,0:T(8,128)S(1)}, f32[8,64]{1,0:T(8,128)S(1)}, u32[]{:S(2)}, u32[]{:S(2)}) collective-permute-start(f32[8,64]{1,0:T(8,128)S(1)} %add.51), channel_id=1, source_target_pairs={{0,8},{1,9},{2,10},{3,11},{4,12},{5,13},{6,14},{7,15},{8,0},{9,1},... | collective-permute-start | bytes 6152 | tf_op jit(solution)/shard_map/ppermute | solution.py:378
  (13 other events, 95.6 us)

commit v3 on v2

--- a/solution.py
+++ b/solution.py
@@ -9,9 +9,9 @@
 
 PARTS = (1, 1, 1, 1)
 GROUP = 4
-STEP_ROWS = 16
-STEP_INS = 8
-TERM_STEP = 512
+STEP_ROWS = 32
+STEP_INS = 16
+TERM_STEP = 1024
 NT = (((1,), (1,)), ((), ()))
 
 

time: 222 us -> 216 us (0.973)
  Pallas kernels: 64.4 us -> 58.1 us
    pallas_call x2, Pallas kernels: 16.4 us -> 13 us  [dress(): pl.pallas_call(functools.partial(dress_kernel, [part * steps for part in...]
    ppermute x23, waiting for transfers between devices: 68.9 us -> 71.8 us  [move(): return lax.ppermute(value, 'tm', route)]
    pallas_call x4, Pallas kernels: 21.8 us -> 19.4 us  [gram(): pl.pallas_call(functools.partial(gram_kernel, count, left_count), grid=(r...]
  transfers between devices with their start and end apart: 27 -> 27, of which waited for: 9 -> 9; matrix products, arithmetic and copies ran while one was open for 5% -> 5% of each run, Pallas kernels for 27% -> 25%
where the time goes in v3:
time: 216 us; the launch traced here: 215 us
  waiting for transfers between devices  81.3 us (38%)
  starting transfers between devices  62.8 us (29%)
  Pallas kernels  58.1 us (27%)
  other arithmetic  8 us (4%)
  local copies, waits for them, and re-layouts  4.37 us (2%)
    ppermute x23, waiting for transfers between devices, move(): return lax.ppermute(value, 'tm', route)  71.8 us
    ppermute x23, starting transfers between devices, move(): return lax.ppermute(value, 'tm', route)  55.5 us
    pallas_call x2, Pallas kernels, box(): pl.pallas_call(functools.partial(box_kernel, [tuple((len(refs) for refs i...  19.7 us
    pallas_call x4, Pallas kernels, gram(): pl.pallas_call(functools.partial(gram_kernel, count, left_count), grid=(r...  19.4 us
    pallas_call x2, Pallas kernels, dress(): pl.pallas_call(functools.partial(dress_kernel, [part * steps for part in...  13 us
    ppermute x4, waiting for transfers between devices, total_over(): lax.ppermute(value, axis, [(i, i ^ distance) for i in range(devices)])  9.55 us
    ppermute x4, starting transfers between devices, total_over(): lax.ppermute(value, axis, [(i, i ^ distance) for i in range(devices)])  7.33 us
    select_n x2, other arithmetic, local(): jnp.where(role == 0, own[half + j][:, :, start:start + length], own[j][:,...  5.45 us
  transfers between devices with their start and end apart: 27, of which 9 were waited for; matrix products, arithmetic and copies ran while one was open for 5% of the time, Pallas kernels for 25%

profile of v3, /device:TPU:0, one launch (start us, length us, event | category | flops | bytes accessed | tf_op | source)
XLA Modules:
  0.0 215.4 jit_solution(2418257193207270896)
XLA Ops:
  3.8 6.5 %collective-permute-start.4 = (bf16[2,32,64,256]{3,2,1,0:T(8,128)(2,1)S(1)}, bf16[2,32,64,256]{3,2,1,0:T(8,128)(2,1)}, u32[]{:S(2)}, u32[]{:S(2)}) collective-permute-start(bf16[2,32,64,256]{3,2,1,0:T(8,128)(2,1)S(1)} %dress.2.refs_0_.refs_4_), channel_id=1, source_target_pairs={{0,12},{3,7},{4,0},{7,11},{8,4},{11,15},{12,8},{15,3},{16,28},{19,... | collective-permute-start | bytes 6291464 | tf_op jit(solution)/shard_map/ppermute | solution.py:395
  11.8 9.8 %dress.3 = (bf16[2,32,64,256]{3,2,1,0:T(8,128)(2,1)}, bf16[2,32,64,256]{3,2,1,0:T(8,128)(2,1)}, bf16[2,32,64,256]{3,2,1,0:T(8,128)(2,1)}) custom-call(bf16[2,32,256,256]{3,2,1,0:T(8,128)(2,1)} %bitcast.45, bf16[2,256,256]{2,1,0:T(8,128)(2,1)} %bitcast.47), custom_call_target="tpu_custom_call" | custom-call | flops 6442450944 | bytes 12582912 | tf_op jit(solution)/shard_map/dress/pallas_call | solution.py:66
  27.0 3.9 %slice_select_fusion = (bf16[2,32,32,256]{3,2,1,0:T(8,128)(2,1)}, bf16[2,32,32,256]{3,2,1,0:T(8,128)(2,1)}) fusion(bf16[2,32,64,256]{3,2,1,0:T(8,128)(2,1)} %get-tuple-element.430.refs_1_.refs_5_, bf16[2,32,64,256]{3,2,1,0:T(8,128)(2,1)} %get-tuple-element.443.refs_3_.refs_7_, pred[]{:T(512)S(6)} %eq.18), kind=kLoop, calls=%fused_computation.2 | loop fusion | flops 1048576 | bytes 6291457 | tf_op jit(solution)/shard_map/jit(_where)/select_n | solution.py:432
  32.5 7.9 %box.11 = f32[8,64]{1,0:T(8,128)} custom-call(s32[5,8]{1,0:T(8,128)} %get-tuple-element.512.ins, f32[4,8]{1,0:T(4,128)} %get-tuple-element.505.scale, bf16[2,32,64,256]{3,2,1,0:T(8,128)(2,1)S(1)} %dress.2.refs_0_.refs_4_, bf16[2,32,64,256]{3,2,1,0:T(8,128)(2,1)} %get-tuple-element.430.refs_1_.refs_5_, ...), custom_call_target="tpu_custom_call" | custom-call | flops 4294967296 | bytes 8388608 | tf_op jit(solution)/shard_map/box/pallas_call | solution.py:207
  43.1 3.6 %collective-permute-start.6 = (bf16[2,32,64,256]{3,2,1,0:T(8,128)(2,1)}, bf16[2,32,64,256]{3,2,1,0:T(8,128)(2,1)}, u32[]{:S(2)}, u32[]{:S(2)}) collective-permute-start(bf16[2,32,64,256]{3,2,1,0:T(8,128)(2,1)} %get-tuple-element.430.refs_1_.refs_5_), channel_id=1, source_target_pairs={{0,12},{3,7},{4,0},{7,11},{8,4},{11,15},{12,8},{15,3},{16,28},{19,... | collective-permute-start | bytes 6291464 | tf_op jit(solution)/shard_map/ppermute | solution.py:395
  46.7 5.3 %conditional.12 = (f32[128,192]{1,0:T(8,128)S(1)}) conditional(s32[]{:T(128)} %convert_element_type.4, (bf16[2,32,64,256]{3,2,1,0:T(8,128)(2,1)S(1)}, bf16[2,32,64,256]{3,2,1,0:T(8,128)(2,1)}, bf16[2,32,64,256]{3,2,1,0:T(8,128)(2,1)}) %tuple.112, (bf16[2,32,64,256]{3,2,1,0:T(8,128)(2,1)S(1)}, bf16[2,32,64,256]{3,2,1,0:T(8,128)(2,1)}, ...), branch_computations={%region_0.1_spmd, %region_1.2_spmd} | conditional | flops 6442450944 | bytes 6389772 | solution.py:507
  47.3 4.7 %gram.15 = f32[128,192]{1,0:T(8,128)S(1)} custom-call(bf16[2,32,64,256]{3,2,1,0:T(8,128)(2,1)S(1)} %get-tuple-element.251.refs_0_, bf16[2,32,64,256]{3,2,1,0:T(8,128)(2,1)} %get-tuple-element.252.refs_1_, bf16[2,32,64,256]{3,2,1,0:T(8,128)(2,1)} %get-tuple-element.253.refs_2_, f32[128,192]{1,0:T(8,128)} %broadcast_in_dim.9.refs_3_), custom_call_target="tpu_custom_call" | custom-call | flops 6442450944 | bytes 6291456 | tf_op jit(solution)/shard_map/cond/branch_1_fun/gram/pallas_call | solution.py:116
  52.0 17.4 %collective-permute-done.2 = bf16[2,32,64,256]{3,2,1,0:T(8,128)(2,1)} collective-permute-done((bf16[2,32,64,256]{3,2,1,0:T(8,128)(2,1)}, bf16[2,32,64,256]{3,2,1,0:T(8,128)(2,1)}, u32[]{:S(2)}, u32[]{:S(2)}) %collective-permute-start.2) | collective-permute-done | bytes 2097184 | tf_op jit(solution)/shard_map/ppermute | solution.py:395
  72.0 3.6 %collective-permute-start.8 = (bf16[2,32,64,256]{3,2,1,0:T(8,128)(2,1)}, bf16[2,32,64,256]{3,2,1,0:T(8,128)(2,1)}, u32[]{:S(2)}, u32[]{:S(2)}) collective-permute-start(bf16[2,32,64,256]{3,2,1,0:T(8,128)(2,1)} %get-tuple-element.431.refs_2_.refs_6_), channel_id=1, source_target_pairs={{0,12},{3,7},{4,0},{7,11},{8,4},{11,15},{12,8},{15,3},{16,28},{19,... | collective-permute-start | bytes 6291464 | tf_op jit(solution)/shard_map/ppermute | solution.py:395
  75.6 4.9 %conditional.13 = (f32[128,192]{1,0:T(8,128)S(1)}) conditional(s32[]{:T(128)} %convert_element_type.4, (bf16[2,32,64,256]{3,2,1,0:T(8,128)(2,1)}, bf16[2,32,64,256]{3,2,1,0:T(8,128)(2,1)}, bf16[2,32,64,256]{3,2,1,0:T(8,128)(2,1)}, f32[128,192]{1,0:T(8,128)S(1)}) %tuple.115, (bf16[2,32,64,256]{3,2,1,0:T(8,128)(2,1)}, ...), branch_computations={%region_2.3_spmd, %region_3.4_spmd} | conditional | flops 6442450944 | bytes 6291464 | solution.py:507
  75.6 4.9 %gram.17 = f32[128,192]{1,0:T(8,128)S(1)} custom-call(bf16[2,32,64,256]{3,2,1,0:T(8,128)(2,1)} %get-tuple-element.258.refs_0_, bf16[2,32,64,256]{3,2,1,0:T(8,128)(2,1)} %get-tuple-element.270.refs_1_, bf16[2,32,64,256]{3,2,1,0:T(8,128)(2,1)} %get-tuple-element.272.refs_2_, f32[128,192]{1,0:T(8,128)S(1)} %get-tuple-element.274.refs_3_), custom_call_target="tpu_custom_call" | custom-call | flops 6442450944 | bytes 6291456 | tf_op jit(solution)/shard_map/cond/branch_1_fun/gram/pallas_call | solution.py:116
  80.5 17.8 %collective-permute-done.1 = bf16[2,32,64,256]{3,2,1,0:T(8,128)(2,1)} collective-permute-done((bf16[2,32,64,256]{3,2,1,0:T(8,128)(2,1)}, bf16[2,32,64,256]{3,2,1,0:T(8,128)(2,1)}, u32[]{:S(2)}, u32[]{:S(2)}) %collective-permute-start.1) | collective-permute-done | bytes 2097184 | tf_op jit(solution)/shard_map/ppermute | solution.py:395
  103.6 3.6 %collective-permute-start.12 = (bf16[2,32,64,256]{3,2,1,0:T(8,128)(2,1)}, bf16[2,32,64,256]{3,2,1,0:T(8,128)(2,1)}, u32[]{:S(2)}, u32[]{:S(2)}) collective-permute-start(bf16[2,32,64,256]{3,2,1,0:T(8,128)(2,1)} %get-tuple-element.443.refs_3_.refs_7_), channel_id=1, source_target_pairs={{0,12},{3,7},{4,0},{7,11},{8,4},{11,15},{12,8},{15,3},{16,28},{19,... | collective-permute-start | bytes 6291464 | tf_op jit(solution)/shard_map/ppermute | solution.py:395
  107.2 5.1 %conditional.14 = (f32[128,192]{1,0:T(8,128)S(1)}) conditional(s32[]{:T(128)} %convert_element_type.4, (bf16[2,32,64,256]{3,2,1,0:T(8,128)(2,1)}, bf16[2,32,64,256]{3,2,1,0:T(8,128)(2,1)}, bf16[2,32,64,256]{3,2,1,0:T(8,128)(2,1)}, f32[128,192]{1,0:T(8,128)S(1)}) %tuple.118, (bf16[2,32,64,256]{3,2,1,0:T(8,128)(2,1)}, ...), branch_computations={%region_4.5_spmd, %region_5.6_spmd} | conditional | flops 6442450944 | bytes 6291464 | solution.py:507
  107.4 4.9 %gram.19 = f32[128,192]{1,0:T(8,128)S(1)} custom-call(bf16[2,32,64,256]{3,2,1,0:T(8,128)(2,1)} %get-tuple-element.280.refs_0_, bf16[2,32,64,256]{3,2,1,0:T(8,128)(2,1)} %get-tuple-element.281.refs_1_, bf16[2,32,64,256]{3,2,1,0:T(8,128)(2,1)} %get-tuple-element.282.refs_2_, f32[128,192]{1,0:T(8,128)S(1)} %get-tuple-element.283.refs_3_), custom_call_target="tpu_custom_call" | custom-call | flops 6442450944 | bytes 6291456 | tf_op jit(solution)/shard_map/cond/branch_1_fun/gram/pallas_call | solution.py:116
  113.0 16.9 %collective-permute-done.10 = bf16[2,32,64,256]{3,2,1,0:T(8,128)(2,1)} collective-permute-done((bf16[2,32,64,256]{3,2,1,0:T(8,128)(2,1)}, bf16[2,32,64,256]{3,2,1,0:T(8,128)(2,1)}, u32[]{:S(2)}, u32[]{:S(2)}) %collective-permute-start.10) | collective-permute-done | bytes 2097184 | tf_op jit(solution)/shard_map/ppermute | solution.py:395
  144.4 4.9 %conditional.16 = (f32[128,192]{1,0:T(8,128)S(1)}) conditional(s32[]{:T(128)} %convert_element_type.4, (bf16[2,32,64,256]{3,2,1,0:T(8,128)(2,1)}, bf16[2,32,64,256]{3,2,1,0:T(8,128)(2,1)}, bf16[2,32,64,256]{3,2,1,0:T(8,128)(2,1)}, f32[128,192]{1,0:T(8,128)S(1)}) %tuple.125, (bf16[2,32,64,256]{3,2,1,0:T(8,128)(2,1)}, ...), branch_computations={%region_8.9_spmd, %region_9.10_spmd} | conditional | flops 6442450944 | bytes 6291464 | solution.py:507
  144.4 4.9 %gram.21 = f32[128,192]{1,0:T(8,128)S(1)} custom-call(bf16[2,32,64,256]{3,2,1,0:T(8,128)(2,1)} %get-tuple-element.298.refs_0_, bf16[2,32,64,256]{3,2,1,0:T(8,128)(2,1)} %get-tuple-element.299.refs_1_, bf16[2,32,64,256]{3,2,1,0:T(8,128)(2,1)} %get-tuple-element.300.refs_2_, f32[128,192]{1,0:T(8,128)S(1)} %get-tuple-element.301.refs_3_), custom_call_target="tpu_custom_call" | custom-call | flops 6442450944 | bytes 6291456 | tf_op jit(solution)/shard_map/cond/branch_1_fun/gram/pallas_call | solution.py:116
  151.9 17.0 %collective-permute-done.16 = bf16[2,32,64,256]{3,2,1,0:T(8,128)(2,1)} collective-permute-done((bf16[2,32,64,256]{3,2,1,0:T(8,128)(2,1)}, bf16[2,32,64,256]{3,2,1,0:T(8,128)(2,1)}, u32[]{:S(2)}, u32[]{:S(2)}) %collective-permute-start.16) | collective-permute-done | bytes 2097184 | tf_op jit(solution)/shard_map/ppermute | solution.py:395
  168.9 5.3 %collective-permute-start.13 = (bf16[2,32,32,256]{3,2,1,0:T(8,128)(2,1)}, bf16[2,32,32,256]{3,2,1,0:T(8,128)(2,1)}, u32[]{:S(2)}, u32[]{:S(2)}) collective-permute-start(bf16[2,32,32,256]{3,2,1,0:T(8,128)(2,1)} %get-tuple-element.463), channel_id=1, source_target_pairs={{0,2},{3,1},{4,6},{7,5},{8,10},{11,9},{12,14},{15,13},{16,18},{19,... | collective-permute-start | bytes 3145736 | tf_op jit(solution)/shard_map/ppermute | solution.py:395
  178.5 11.8 %conditional.17 = (f32[8,64]{1,0:T(8,128)S(1)}) conditional(s32[]{:T(128)} %convert_element_type.4, (s32[5,8]{1,0:T(8,128)S(1)}, f32[4,8]{1,0:T(4,128)S(1)}, bf16[2,32,64,256]{3,2,1,0:T(8,128)(2,1)S(1)}, bf16[2,32,64,256]{3,2,1,0:T(8,128)(2,1)}, bf16[2,32,64,256]{3,2,1,0:T(8,128)(2,1)}, /*index=5*/bf16[2,32,64,256]{3,2,1,0:T(8,128)(2,1)}, ...), branch_computations={%region_10.11_spmd, %region_11.12_spmd} | conditional | flops 8589934592 | bytes 16777224 | solution.py:524
  178.5 11.8 %box.8 = f32[8,64]{1,0:T(8,128)S(1)} custom-call(s32[5,16]{1,0:T(8,128)S(1)} %get-tuple-element.312.ins, f32[4,16]{1,0:T(4,128)S(1)} %get-tuple-element.313.scale, bf16[2,32,64,256]{3,2,1,0:T(8,128)(2,1)S(1)} %get-tuple-element.314.refs_0_, bf16[2,32,64,256]{3,2,1,0:T(8,128)(2,1)} %get-tuple-element.315.refs_1_, ...), custom_call_target="tpu_custom_call" | custom-call | flops 8589934592 | bytes 16777216 | tf_op jit(solution)/shard_map/cond/branch_1_fun/box/pallas_call | solution.py:207
  197.8 4.3 %collective-permute-start.23 = (f32[8,64]{1,0:T(8,128)S(1)}, f32[8,64]{1,0:T(8,128)S(1)}, u32[]{:S(2)}, u32[]{:S(2)}) collective-permute-start(f32[8,64]{1,0:T(8,128)S(1)} %add_add_fusion.2), channel_id=1, source_target_pairs={{0,1},{1,0},{2,3},{3,2},{4,5},{5,4},{6,7},{7,6},{8,9},{9,8},{10,11... | collective-permute-start | bytes 6152 | tf_op jit(solution)/shard_map/ppermute | solution.py:378
  206.6 3.6 %collective-permute-done.25 = f32[8,64]{1,0:T(8,128)S(1)} collective-permute-done((f32[8,64]{1,0:T(8,128)S(1)}, f32[8,64]{1,0:T(8,128)S(1)}, u32[]{:S(2)}, u32[]{:S(2)}) %collective-permute-start.25) | collective-permute-done | bytes 2080 | tf_op jit(solution)/shard_map/ppermute | solution.py:378
  (118 shorter events, 62.4 us)
Async XLA Ops:
  3.2 37.1 %collective-permute-start = (bf16[2,32,64,256]{3,2,1,0:T(8,128)(2,1)S(1)}, bf16[2,32,64,256]{3,2,1,0:T(8,128)(2,1)}, u32[]{:S(2)}, u32[]{:S(2)}) collective-permute-start(bf16[2,32,64,256]{3,2,1,0:T(8,128)(2,1)S(1)} %dress.2.refs_0_.refs_4_), channel_id=1, source_target_pairs={{0,1},{1,3},{2,0},{3,2},{4,5},{5,7},{6,4},{7,6},{8,9},{9,11},{10,8... | collective-permute-start | bytes 6291464 | tf_op jit(solution)/shard_map/ppermute | solution.py:395
  3.8 42.9 %collective-permute-start.4 = (bf16[2,32,64,256]{3,2,1,0:T(8,128)(2,1)S(1)}, bf16[2,32,64,256]{3,2,1,0:T(8,128)(2,1)}, u32[]{:S(2)}, u32[]{:S(2)}) collective-permute-start(bf16[2,32,64,256]{3,2,1,0:T(8,128)(2,1)S(1)} %dress.2.refs_0_.refs_4_), channel_id=1, source_target_pairs={{0,12},{3,7},{4,0},{7,11},{8,4},{11,15},{12,8},{15,3},{16,28},{19,... | collective-permute-start | bytes 6291464 | tf_op jit(solution)/shard_map/ppermute | solution.py:395
  40.4 6.3 %collective-permute-start.3 = (bf16[2,32,64,256]{3,2,1,0:T(8,128)(2,1)}, bf16[2,32,64,256]{3,2,1,0:T(8,128)(2,1)}, u32[]{:S(2)}, u32[]{:S(2)}) collective-permute-start(bf16[2,32,64,256]{3,2,1,0:T(8,128)(2,1)} %collective-permute-done), channel_id=1, source_target_pairs={{0,1},{3,2},{4,5},{7,6},{8,9},{11,10},{12,13},{15,14},{16,17},{19,... | collective-permute-start | bytes 6291464 | tf_op jit(solution)/shard_map/ppermute | solution.py:395
  43.1 26.4 %collective-permute-start.2 = (bf16[2,32,64,256]{3,2,1,0:T(8,128)(2,1)}, bf16[2,32,64,256]{3,2,1,0:T(8,128)(2,1)}, u32[]{:S(2)}, u32[]{:S(2)}) collective-permute-start(bf16[2,32,64,256]{3,2,1,0:T(8,128)(2,1)} %get-tuple-element.430.refs_1_.refs_5_), channel_id=1, source_target_pairs={{0,1},{1,3},{2,0},{3,2},{4,5},{5,7},{6,4},{7,6},{8,9},{9,11},{10,8... | collective-permute-start | bytes 6291464 | tf_op jit(solution)/shard_map/ppermute | solution.py:395
  43.1 32.5 %collective-permute-start.6 = (bf16[2,32,64,256]{3,2,1,0:T(8,128)(2,1)}, bf16[2,32,64,256]{3,2,1,0:T(8,128)(2,1)}, u32[]{:S(2)}, u32[]{:S(2)}) collective-permute-start(bf16[2,32,64,256]{3,2,1,0:T(8,128)(2,1)} %get-tuple-element.430.refs_1_.refs_5_), channel_id=1, source_target_pairs={{0,12},{3,7},{4,0},{7,11},{8,4},{11,15},{12,8},{15,3},{16,28},{19,... | collective-permute-start | bytes 6291464 | tf_op jit(solution)/shard_map/ppermute | solution.py:395
  69.4 6.2 %collective-permute-start.5 = (bf16[2,32,64,256]{3,2,1,0:T(8,128)(2,1)}, bf16[2,32,64,256]{3,2,1,0:T(8,128)(2,1)}, u32[]{:S(2)}, u32[]{:S(2)}) collective-permute-start(bf16[2,32,64,256]{3,2,1,0:T(8,128)(2,1)} %collective-permute-done.2), channel_id=1, source_target_pairs={{0,1},{3,2},{4,5},{7,6},{8,9},{11,10},{12,13},{15,14},{16,17},{19,... | collective-permute-start | bytes 6291464 | tf_op jit(solution)/shard_map/ppermute | solution.py:395
  72.0 26.4 %collective-permute-start.1 = (bf16[2,32,64,256]{3,2,1,0:T(8,128)(2,1)}, bf16[2,32,64,256]{3,2,1,0:T(8,128)(2,1)}, u32[]{:S(2)}, u32[]{:S(2)}) collective-permute-start(bf16[2,32,64,256]{3,2,1,0:T(8,128)(2,1)} %get-tuple-element.431.refs_2_.refs_6_), channel_id=1, source_target_pairs={{0,1},{1,3},{2,0},{3,2},{4,5},{5,7},{6,4},{7,6},{8,9},{9,11},{10,8... | collective-permute-start | bytes 6291464 | tf_op jit(solution)/shard_map/ppermute | solution.py:395
  72.0 35.2 %collective-permute-start.8 = (bf16[2,32,64,256]{3,2,1,0:T(8,128)(2,1)}, bf16[2,32,64,256]{3,2,1,0:T(8,128)(2,1)}, u32[]{:S(2)}, u32[]{:S(2)}) collective-permute-start(bf16[2,32,64,256]{3,2,1,0:T(8,128)(2,1)} %get-tuple-element.431.refs_2_.refs_6_), channel_id=1, source_target_pairs={{0,12},{3,7},{4,0},{7,11},{8,4},{11,15},{12,8},{15,3},{16,28},{19,... | collective-permute-start | bytes 6291464 | tf_op jit(solution)/shard_map/ppermute | solution.py:395
  98.3 8.8 %collective-permute-start.7 = (bf16[2,32,64,256]{3,2,1,0:T(8,128)(2,1)}, bf16[2,32,64,256]{3,2,1,0:T(8,128)(2,1)}, u32[]{:S(2)}, u32[]{:S(2)}) collective-permute-start(bf16[2,32,64,256]{3,2,1,0:T(8,128)(2,1)} %collective-permute-done.1), channel_id=1, source_target_pairs={{0,1},{3,2},{4,5},{7,6},{8,9},{11,10},{12,13},{15,14},{16,17},{19,... | collective-permute-start | bytes 6291464 | tf_op jit(solution)/shard_map/ppermute | solution.py:395
  101.0 11.3 %collective-permute-start.9 = (bf16[2,32,64,256]{3,2,1,0:T(8,128)(2,1)}, bf16[2,32,64,256]{3,2,1,0:T(8,128)(2,1)}, u32[]{:S(2)}, u32[]{:S(2)}) collective-permute-start(bf16[2,32,64,256]{3,2,1,0:T(8,128)(2,1)} %get-tuple-element.443.refs_3_.refs_7_), channel_id=1, source_target_pairs={{0,1},{3,2},{4,5},{7,6},{8,9},{11,10},{12,13},{15,14},{16,17},{19,... | collective-permute-start | bytes 6291464 | tf_op jit(solution)/shard_map/ppermute | solution.py:395
  103.6 26.4 %collective-permute-start.10 = (bf16[2,32,64,256]{3,2,1,0:T(8,128)(2,1)}, bf16[2,32,64,256]{3,2,1,0:T(8,128)(2,1)}, u32[]{:S(2)}, u32[]{:S(2)}) collective-permute-start(bf16[2,32,64,256]{3,2,1,0:T(8,128)(2,1)} %get-tuple-element.443.refs_3_.refs_7_), channel_id=1, source_target_pairs={{0,1},{1,3},{2,0},{3,2},{4,5},{5,7},{6,4},{7,6},{8,9},{9,11},{10,8... | collective-permute-start | bytes 6291464 | tf_op jit(solution)/shard_map/ppermute | solution.py:395
  103.6 35.5 %collective-permute-start.12 = (bf16[2,32,64,256]{3,2,1,0:T(8,128)(2,1)}, bf16[2,32,64,256]{3,2,1,0:T(8,128)(2,1)}, u32[]{:S(2)}, u32[]{:S(2)}) collective-permute-start(bf16[2,32,64,256]{3,2,1,0:T(8,128)(2,1)} %get-tuple-element.443.refs_3_.refs_7_), channel_id=1, source_target_pairs={{0,12},{3,7},{4,0},{7,11},{8,4},{11,15},{12,8},{15,3},{16,28},{19,... | collective-permute-start | bytes 6291464 | tf_op jit(solution)/shard_map/ppermute | solution.py:395
  129.9 11.8 %collective-permute-start.11 = (bf16[2,32,64,256]{3,2,1,0:T(8,128)(2,1)}, bf16[2,32,64,256]{3,2,1,0:T(8,128)(2,1)}, u32[]{:S(2)}, u32[]{:S(2)}) collective-permute-start(bf16[2,32,64,256]{3,2,1,0:T(8,128)(2,1)} %collective-permute-done.10), channel_id=1, source_target_pairs={{0,1},{3,2},{4,5},{7,6},{8,9},{11,10},{12,13},{15,14},{16,17},{19,... | collective-permute-start | bytes 6291464 | tf_op jit(solution)/shard_map/ppermute | solution.py:395
  132.6 16.7 %collective-permute-start.15 = (bf16[2,32,32,256]{3,2,1,0:T(8,128)(2,1)}, bf16[2,32,32,256]{3,2,1,0:T(8,128)(2,1)S(1)}, u32[]{:S(2)}, u32[]{:S(2)}) collective-permute-start(bf16[2,32,32,256]{3,2,1,0:T(8,128)(2,1)} %get-tuple-element.466), channel_id=1, source_target_pairs={{0,2},{3,1},{4,6},{7,5},{8,10},{11,9},{12,14},{15,13},{16,18},{19,... | collective-permute-start | bytes 3145736 | tf_op jit(solution)/shard_map/ppermute | solution.py:395
  133.9 35.0 %collective-permute-start.16 = (bf16[2,32,64,256]{3,2,1,0:T(8,128)(2,1)}, bf16[2,32,64,256]{3,2,1,0:T(8,128)(2,1)}, u32[]{:S(2)}, u32[]{:S(2)}) collective-permute-start(bf16[2,32,64,256]{3,2,1,0:T(8,128)(2,1)} %broadcast_select_fusion), channel_id=1, source_target_pairs={{0,2},{3,1},{4,6},{7,5},{8,10},{11,9},{12,14},{15,13},{16,18},{19,... | collective-permute-start | bytes 6291464 | tf_op jit(solution)/shard_map/ppermute | solution.py:395
  136.5 37.8 %collective-permute-start.17 = (bf16[2,32,64,256]{3,2,1,0:T(8,128)(2,1)}, bf16[2,32,64,256]{3,2,1,0:T(8,128)(2,1)}, u32[]{:S(2)}, u32[]{:S(2)}) collective-permute-start(bf16[2,32,64,256]{3,2,1,0:T(8,128)(2,1)} %collective-permute-done.4), channel_id=1, source_target_pairs={{0,1},{3,2},{4,5},{7,6},{8,9},{11,10},{12,13},{15,14},{16,17},{19,... | collective-permute-start | bytes 6291464 | tf_op jit(solution)/shard_map/ppermute | solution.py:395
  139.1 37.2 %collective-permute-start.18 = (bf16[2,32,64,256]{3,2,1,0:T(8,128)(2,1)}, bf16[2,32,64,256]{3,2,1,0:T(8,128)(2,1)}, u32[]{:S(2)}, u32[]{:S(2)}) collective-permute-start(bf16[2,32,64,256]{3,2,1,0:T(8,128)(2,1)} %collective-permute-done.8), channel_id=1, source_target_pairs={{0,1},{3,2},{4,5},{7,6},{8,9},{11,10},{12,13},{15,14},{16,17},{19,... | collective-permute-start | bytes 6291464 | tf_op jit(solution)/shard_map/ppermute | solution.py:395
  141.8 52.0 %collective-permute-start.14 = (bf16[2,32,64,256]{3,2,1,0:T(8,128)(2,1)}, bf16[2,32,64,256]{3,2,1,0:T(8,128)(2,1)}, u32[]{:S(2)}, u32[]{:S(2)}) collective-permute-start(bf16[2,32,64,256]{3,2,1,0:T(8,128)(2,1)} %collective-permute-done.6), channel_id=1, source_target_pairs={{0,1},{3,2},{4,5},{7,6},{8,9},{11,10},{12,13},{15,14},{16,17},{19,... | collective-permute-start | bytes 6291464 | tf_op jit(solution)/shard_map/ppermute | solution.py:395
  149.3 44.5 %collective-permute-start.19 = (bf16[2,32,64,256]{3,2,1,0:T(8,128)(2,1)}, bf16[2,32,64,256]{3,2,1,0:T(8,128)(2,1)}, u32[]{:S(2)}, u32[]{:S(2)}) collective-permute-start(bf16[2,32,64,256]{3,2,1,0:T(8,128)(2,1)} %collective-permute-done.12), channel_id=1, source_target_pairs={{0,1},{3,2},{4,5},{7,6},{8,9},{11,10},{12,13},{15,14},{16,17},{19,... | collective-permute-start | bytes 6291464 | tf_op jit(solution)/shard_map/ppermute | solution.py:395
  168.9 24.9 %collective-permute-start.13 = (bf16[2,32,32,256]{3,2,1,0:T(8,128)(2,1)}, bf16[2,32,32,256]{3,2,1,0:T(8,128)(2,1)}, u32[]{:S(2)}, u32[]{:S(2)}) collective-permute-start(bf16[2,32,32,256]{3,2,1,0:T(8,128)(2,1)} %get-tuple-element.463), channel_id=1, source_target_pairs={{0,2},{3,1},{4,6},{7,5},{8,10},{11,9},{12,14},{15,13},{16,18},{19,... | collective-permute-start | bytes 3145736 | tf_op jit(solution)/shard_map/ppermute | solution.py:395
  174.3 20.2 %collective-permute-start.20 = (bf16[1,2,4,128,256]{4,3,2,1,0:T(8,128)(2,1)}, bf16[1,2,4,128,256]{4,3,2,1,0:T(8,128)(2,1)}, u32[]{:S(2)}, u32[]{:S(2)}) collective-permute-start(bf16[1,2,4,128,256]{4,3,2,1,0:T(8,128)(2,1)} %get-tuple-element.476), channel_id=1, source_target_pairs={{0,2},{3,1},{4,6},{7,5},{8,10},{11,9},{12,14},{15,13},{16,18},{19,... | collective-permute-start | bytes 1572872 | tf_op jit(solution)/shard_map/ppermute | solution.py:395
  176.4 20.8 %collective-permute-start.22 = (bf16[1,2,4,128,256]{4,3,2,1,0:T(8,128)(2,1)}, bf16[1,2,4,128,256]{4,3,2,1,0:T(8,128)(2,1)}, u32[]{:S(2)}, u32[]{:S(2)}) collective-permute-start(bf16[1,2,4,128,256]{4,3,2,1,0:T(8,128)(2,1)} %get-tuple-element.486), channel_id=1, source_target_pairs={{0,2},{3,1},{4,6},{7,5},{8,10},{11,9},{12,14},{15,13},{16,18},{19,... | collective-permute-start | bytes 1572872 | tf_op jit(solution)/shard_map/ppermute | solution.py:395
  197.8 5.2 %collective-permute-start.23 = (f32[8,64]{1,0:T(8,128)S(1)}, f32[8,64]{1,0:T(8,128)S(1)}, u32[]{:S(2)}, u32[]{:S(2)}) collective-permute-start(f32[8,64]{1,0:T(8,128)S(1)} %add_add_fusion.2), channel_id=1, source_target_pairs={{0,1},{1,0},{2,3},{3,2},{4,5},{5,4},{6,7},{7,6},{8,9},{9,8},{10,11... | collective-permute-start | bytes 6152 | tf_op jit(solution)/shard_map/ppermute | solution.py:378
  210.2 4.5 %collective-permute-start.26 = (f32[8,64]{1,0:T(8,128)S(1)}, f32[8,64]{1,0:T(8,128)S(1)}, u32[]{:S(2)}, u32[]{:S(2)}) collective-permute-start(f32[8,64]{1,0:T(8,128)S(1)} %add.51), channel_id=1, source_target_pairs={{0,8},{1,9},{2,10},{3,11},{4,12},{5,13},{6,14},{7,15},{8,0},{9,1},... | collective-permute-start | bytes 6152 | tf_op jit(solution)/shard_map/ppermute | solution.py:378
  (13 other events, 90.1 us)
